TPU v7x, 512 devices: a whole 4x8x8 slice. The times are simulated.
512 devices in a mesh: context: 64 (over z, y), tensor: 8 (over x, core).
Axes of the slice: x: 4, y: 8, z: 8, core: 2. Of those that a mesh axis runs over, the one named last changes fastest.
Arguments:
- query_proj: bfloat16 [8192, 8192], P('context', 'tensor'), may hold values from -6 to 6
- key_proj: bfloat16 [8192, 8192], P('context', 'tensor'), may hold values from -6 to 6
- value_proj: bfloat16 [8192, 8192], P('context', 'tensor'), may hold values from -6 to 6
- short_filter: float32 [3, 7, 8192], P(None, None, 'tensor'), may hold values from -2 to 2
- residues: float32 [16, 8192], P(None, 'tensor'), may hold values from -1.5 to 1.5
- decay: float32 [16, 8192], P(None, 'tensor'), may hold values from 0.00012207031 to 0.033333335
- skip_gain: float32 [8192], P('tensor'), may hold values from -6 to 6
- residual: bfloat16 [8192, 8192], P('context', 'tensor'), may hold values from -50 to 50
- norm_gain: float32 [8192], P('tensor'), may hold values from 0.5 to 1.5
Outputs:
- mixed: bfloat16 [8192, 8192], P('context', 'tensor')
- normed: bfloat16 [8192, 8192], P('context', 'tensor')
All inputs are finite; a program needn't handle non-finite values.
Results may differ from a plain program's by a relative error of at most 0.014.
Values may be sent and summed in bfloat16 or wider, within the bound.
No kernel may reach another device: no remote copies, remote signals or barrier semaphores. Data moves between devices by JAX's collectives and lax.ppermute only.
A program may use at most 64 MiB of HBM per device.

v0:
```python
import jax
import jax.numpy as jnp
from jax import lax
from jax.experimental import pallas as pl
from jax.experimental.pallas import tpu as pltpu
from jax.sharding import Mesh, PartitionSpec as P

D = 8192
ORDER = 16
TAPS = 7
ROWS = 128
LANES = 128
GROUPS = 8
BLOCK = 8

f32 = jnp.float32
bf16 = jnp.bfloat16


def stack_rows(dst, src, first, rows, at, step=16):
    for r in range(0, rows, step):
        for j in range(GROUPS):
            tile = src[first + r : first + r + step, j * LANES : (j + 1) * LANES]
            dst[pl.ds((at + r) * GROUPS + j, step, stride=GROUPS), :] = tile.astype(f32)


def stack_taps(dst, taps, which):
    for j in range(GROUPS):
        dst[pl.ds(j, TAPS, stride=GROUPS), :] = taps[which, :, j * LANES : (j + 1) * LANES]


def row(ref, n):
    return ref[pl.ds(pl.multiple_of(n * GROUPS, GROUPS), GROUPS), :]


def put(ref, n, value):
    ref[pl.ds(pl.multiple_of(n * GROUPS, GROUPS), GROUPS), :] = value


def conv(ref, taps, n0, count):
    rows = [row(ref, n0 + 8 - (TAPS - 1) + i) for i in range(count + TAPS - 1)]
    out = []
    for i in range(count):
        total = rows[i + TAPS - 1] * taps[0]
        for j in range(1, TAPS):
            total = total + rows[i + TAPS - 1 - j] * taps[j]
        out.append(total)
    return out


def rows_of(ref, count):
    return [row(ref, m) for m in range(count)]


def total_of(values):
    values = list(values)
    while len(values) > 1:
        values = [a + b for a, b in zip(values[::2], values[1::2])] + (
            [values[-1]] if len(values) % 2 else []
        )
    return values[0]


def call(body, name, outs, scratch, count, scalars=0):
    spec = pl.BlockSpec(memory_space=pltpu.VMEM)
    small = pl.BlockSpec(memory_space=pltpu.SMEM)
    return pl.pallas_call(
        body,
        name=name,
        out_shape=tuple(jax.ShapeDtypeStruct(s, t) for s, t in outs),
        in_specs=[small] * scalars + [spec] * (count - scalars),
        out_specs=tuple(spec for _ in outs),
        scratch_shapes=scratch,
        compiler_params=pltpu.CompilerParams(vmem_limit_bytes=32 << 20),
    )


def local_state(k_ref, v_ref, f_ref, d_ref, u_ref, state_ref, kt, vt, kf, vf, dt):
    stack_taps(kf, f_ref, 1)
    stack_taps(vf, f_ref, 2)
    stack_rows(dt, d_ref, 0, ORDER, 0)
    stack_rows(kt, k_ref, 0, ROWS, 8)
    stack_rows(vt, v_ref, 0, ROWS, 8)
    ktaps, vtaps = rows_of(kf, TAPS), rows_of(vf, TAPS)
    pole = [jnp.exp(-d) for d in rows_of(dt, ORDER)]

    def products(n0, count):
        us = [a * b for a, b in zip(conv(kt, ktaps, n0, count), conv(vt, vtaps, n0, count))]
        for i, u in enumerate(us):
            put(u_ref, n0 + i, u)
        return us

    def advance(state, us):
        for u in us:
            state = [p * s + u for p, s in zip(pole, state)]
        return state

    skip = TAPS - 1
    us = products(skip, BLOCK - skip)
    state = advance([us[0]] * ORDER, us[1:])

    def step(b, state):
        return tuple(advance(list(state), products(b * BLOCK, BLOCK)))

    state = lax.fori_loop(1, ROWS // BLOCK, step, tuple(state))
    for m in range(ORDER):
        put(state_ref, m, state[m])


def edge_state(halo_ref, k_ref, v_ref, f_ref, d_ref, state_ref, out_ref, u_ref, kt, vt, kf, vf, dt):
    stack_taps(kf, f_ref, 1)
    stack_taps(vf, f_ref, 2)
    stack_rows(dt, d_ref, 0, ORDER, 0)
    stack_rows(kt, halo_ref, 8, 8, 0, 8)
    stack_rows(vt, halo_ref, 16, 8, 0, 8)
    stack_rows(kt, k_ref, 0, 8, 8, 8)
    stack_rows(vt, v_ref, 0, 8, 8, 8)
    count = TAPS - 1
    ks = conv(kt, rows_of(kf, TAPS), 0, count)
    vs = conv(vt, rows_of(vf, TAPS), 0, count)
    us = [a * b for a, b in zip(ks, vs)]
    for i, u in enumerate(us):
        put(u_ref, i, u)
    for m in range(0, ORDER, 2):
        pair = []
        for i in (m, m + 1):
            d = row(dt, i)
            p = jnp.exp(-d)
            s = us[0]
            for u in us[1:]:
                s = p * s + u
            pair.append(row(state_ref, i) + jnp.exp(-(ROWS - count) * d) * s)
        both = jnp.concatenate(pair, axis=0).astype(bf16)
        for copy in range(8):
            out_ref[(copy * ORDER + m) * GROUPS : (copy * ORDER + m + 2) * GROUPS, :] = both


def own_part(
    halo_ref, q_ref, u_ref, edge_ref, f_ref, d_ref, w_ref, skip_ref, qc_ref, g_ref, qt, qf, dt, wt, st
):
    stack_taps(qf, f_ref, 0)
    stack_rows(dt, d_ref, 0, ORDER, 0)
    stack_rows(wt, w_ref, 0, ORDER, 0)
    for j in range(GROUPS):
        st[j : j + 1, :] = skip_ref[0:1, j * LANES : (j + 1) * LANES]
    stack_rows(qt, halo_ref, 0, 8, 0, 8)
    stack_rows(qt, q_ref, 0, ROWS, 8)
    taps = rows_of(qf, TAPS)
    pole = [jnp.exp(-d) for d in rows_of(dt, ORDER)]
    weight = rows_of(wt, ORDER)
    gain = st[...]

    def advance(n0, state, us):
        for i, u in enumerate(us):
            state = [p * s + u for p, s in zip(pole, state)]
            put(g_ref, n0 + i, total_of([w * s for w, s in zip(weight, state)] + [gain * u]))
        return state

    def queries(n0):
        for i, c in enumerate(conv(qt, taps, n0, BLOCK)):
            put(qc_ref, n0 + i, c)

    edge = TAPS - 1
    us = rows_of(edge_ref, edge) + [row(u_ref, n) for n in range(edge, BLOCK)]
    zero = jnp.zeros((GROUPS, LANES), f32)
    state = advance(0, [zero] * ORDER, us)
    queries(0)

    def step(b, state):
        n0 = b * BLOCK
        queries(n0)
        return tuple(advance(n0, list(state), [row(u_ref, n0 + i) for i in range(BLOCK)]))

    lax.fori_loop(1, ROWS // BLOCK, step, tuple(state))


def load_pair(ref, block, m):
    both = ref[(block * ORDER + m) * GROUPS : (block * ORDER + m + 2) * GROUPS, :].astype(f32)
    return both[:GROUPS], both[GROUPS:]


def scan_blocks(ref, m, steps, index):
    zero = jnp.zeros((GROUPS, LANES), f32)
    total, before = [zero, zero], [zero, zero]
    for b in range(8):
        here = index == b
        before = [jnp.where(here, t, o) for t, o in zip(total, before)]
        total = [s * t + x for s, t, x in zip(steps, total, load_pair(ref, b, m))]
    return before, total


def scan_near(at_ref, got_ref, d_ref, out_ref, before_ref, dt):
    stack_rows(dt, d_ref, 0, ORDER, 0)
    index = at_ref[1]
    for m in range(0, ORDER, 2):
        steps = [jnp.exp(-float(ROWS) * row(dt, i)) for i in (m, m + 1)]
        before, total = scan_blocks(got_ref, m, steps, index)
        for i in range(2):
            put(before_ref, m + i, before[i])
        both = jnp.concatenate(total, axis=0).astype(bf16)
        for copy in range(8):
            out_ref[(copy * ORDER + m) * GROUPS : (copy * ORDER + m + 2) * GROUPS, :] = both


def finish(
    at_ref, got_ref, before_ref, d_ref, w_ref, qc_ref, g_ref, residual_ref, gain_ref,
    mixed_ref, scaled_ref, squares_ref, dt, wt, st, mt, sq,
):
    stack_rows(dt, d_ref, 0, ORDER, 0)
    stack_rows(wt, w_ref, 0, ORDER, 0)
    far, near = at_ref[0], at_ref[1].astype(f32)
    for m in range(0, ORDER, 2):
        rates = [row(dt, i) for i in (m, m + 1)]
        steps = [jnp.exp(-float(8 * ROWS) * d) for d in rates]
        before, _ = scan_blocks(got_ref, m, steps, far)
        for i in range(2):
            entry = row(before_ref, m + i) + jnp.exp(-float(ROWS) * near * rates[i]) * before[i]
            put(st, m + i, row(wt, m + i) * entry)
    pole = [jnp.exp(-d) for d in rows_of(dt, ORDER)]
    count = 16

    def step(b, state):
        n0 = b * count
        state = list(state)
        for i in range(count):
            state = [p * s for p, s in zip(pole, state)]
            value = row(qc_ref, n0 + i) * (row(g_ref, n0 + i) + total_of(state))
            mt[i * GROUPS : (i + 1) * GROUPS, :] = value
        at = pl.ds(pl.multiple_of(n0, count), count)
        squares = None
        for j in range(GROUPS):
            lanes = slice(j * LANES, (j + 1) * LANES)
            tile = mt[pl.ds(j, count, stride=GROUPS), :].astype(bf16)
            mixed_ref[at, lanes] = tile
            summed = residual_ref[at, lanes].astype(f32) + tile.astype(f32)
            scaled_ref[at, lanes] = summed * gain_ref[0:1, lanes]
            part = summed * summed
            squares = part if squares is None else squares + part
        sq[at, :] = squares
        return tuple(state)

    lax.fori_loop(0, ROWS // count, step, tuple(rows_of(st, ORDER)))
    squares_ref[...] = lax.dot_general(
        jnp.ones((8, LANES), f32), sq[...], (((1,), (1,)), ((), ())),
        precision=lax.Precision.HIGHEST, preferred_element_type=f32,
    )


def normalise(scaled_ref, squares_ref, out_ref):
    total = lax.dot_general(
        squares_ref[...], jnp.ones((8, LANES), f32), (((0,), (0,)), ((), ())),
        precision=lax.Precision.HIGHEST, preferred_element_type=f32,
    )
    factor = lax.rsqrt(total / D + 1e-05)
    for j in range(GROUPS):
        lanes = slice(j * LANES, (j + 1) * LANES)
        out_ref[:, lanes] = (scaled_ref[:, lanes] * factor).astype(bf16)


def shards(query, key, value, short_filter, residues, decay, skip_gain, residual, norm_gain):
    stacked = ((ROWS + 8) * GROUPS, LANES)
    modes = (ORDER * GROUPS, LANES)
    taps = (8 * GROUPS, LANES)
    blocks = (8 * ORDER * GROUPS, LANES)
    whole = (ROWS * GROUPS, LANES)
    vmem = pltpu.VMEM

    weight = residues * jnp.sqrt(-jnp.expm1(-2.0 * decay))
    at = jnp.stack([lax.axis_index("z"), lax.axis_index("y")]).astype(jnp.int32)
    tails = jnp.concatenate([x[ROWS - 8 :] for x in (query, key, value)], axis=0)
    halo = lax.ppermute(tails, ("z", "y"), [(i, i + 1) for i in range(63)])

    u, clean = call(
        local_state, "local_state", [(whole, f32), (modes, f32)],
        [vmem(stacked, f32)] * 2 + [vmem(taps, f32)] * 2 + [vmem(modes, f32)],
        4,
    )(key, value, short_filter, decay)
    sent, edge = call(
        edge_state, "edge_state", [(blocks, bf16), (taps, f32)],
        [vmem((16 * GROUPS, LANES), f32)] * 2 + [vmem(taps, f32)] * 2 + [vmem(modes, f32)],
        6,
    )(halo, key[:16], value[:16], short_filter, decay, clean)
    near = lax.all_to_all(sent, "y", 0, 0, tiled=True)
    qc, own = call(
        own_part, "own_part", [(whole, f32)] * 2,
        [vmem(stacked, f32), vmem(taps, f32)] + [vmem(modes, f32)] * 2 + [vmem((GROUPS, LANES), f32)],
        8,
    )(halo, query, u, edge, short_filter, decay, weight, skip_gain[None])
    totals, before = call(
        scan_near, "scan_near", [(blocks, bf16), (modes, f32)], [vmem(modes, f32)], 3, 1,
    )(at, near, decay)
    far = lax.all_to_all(totals, "z", 0, 0, tiled=True)
    mixed, scaled, squares = call(
        finish, "finish",
        [((ROWS, 1024), bf16), ((ROWS, 1024), f32), ((8, LANES), f32)],
        [vmem(modes, f32)] * 3 + [vmem((16 * GROUPS, LANES), f32), vmem((ROWS, LANES), f32)],
        9, 1,
    )(at, far, before, decay, weight, qc, own, residual, norm_gain[None])
    gathered = lax.all_to_all(squares, "tensor", 0, 0, tiled=True)
    (normed,) = call(normalise, "normalise", [((ROWS, 1024), bf16)], [], 2)(scaled, gathered)
    return mixed, normed


def solution(mesh):
    context = ("z", "y")
    split = Mesh(mesh.devices.reshape(8, 8, 8), ("z", "y", "tensor"))
    rows = P(context, "tensor")
    in_specs = (
        rows, rows, rows, P(None, None, "tensor"), P(None, "tensor"), P(None, "tensor"),
        P("tensor"), rows, P("tensor"),
    )
    return jax.shard_map(shards, mesh=split, in_specs=in_specs, out_specs=(rows, rows), check_vma=False)
```

profile of v0, /device:TPU:1, one launch (start us, length us, event | category | flops | bytes accessed | tf_op | source)
XLA Modules:
  0.0 64.5 jit_solution(13385977148300868525)
XLA Ops:
  0.6 0.0 slice-start.2
  0.6 0.0 slice-start
  0.7 0.7 %slice-done.2 = bf16[8,1024]{1,0:T(8,128)(2,1)S(1)} async-done(((bf16[128,1024]{1,0:T(8,128)(2,1)}), bf16[8,1024]{1,0:T(8,128)(2,1)S(1)}, s32[]{:S(2)}) %slice-start.2) | async-done | bytes 16408 | tf_op jit(solution)/shard_map/slice | solution.py:270
  1.4 0.0 slice-done
  1.4 0.0 slice-done.1
  1.4 4.2 %collective-permute-start = (bf16[24,1024]{1,0:T(8,128)(2,1)S(1)}, bf16[24,1024]{1,0:T(8,128)(2,1)S(1)}, u32[]{:S(2)}, u32[]{:S(2)}) collective-permute-start(bf16[24,1024]{1,0:T(8,128)(2,1)S(1)} %pad_maximum_fusion), channel_id=1, source_target_pairs={{0,8},{8,16},{16,24},{24,32},{32,40},{40,48},{48,56},{56,64},{64,7... | collective-permute-start | bytes 147464 | tf_op jit(solution)/shard_map/ppermute | solution.py:271
  5.6 0.8 %slice.18.k_ref = bf16[16,1024]{1,0:T(8,128)(2,1)S(1)} slice(bf16[128,1024]{1,0:T(8,128)(2,1)} %k_ref.1), slice={[0:16], [0:1024]} | slice | bytes 65536 | tf_op jit(solution)/shard_map/slice | solution.py:282
  6.3 0.8 %slice.19.v_ref = bf16[16,1024]{1,0:T(8,128)(2,1)S(1)} slice(bf16[128,1024]{1,0:T(8,128)(2,1)} %v_ref.1), slice={[0:16], [0:1024]} | slice | bytes 65536 | tf_op jit(solution)/shard_map/slice | solution.py:282
  7.1 0.9 %copy-done.2 = bf16[128,1024]{1,0:T(8,128)(2,1)S(1)} copy-done((bf16[128,1024]{1,0:T(8,128)(2,1)S(1)}, bf16[128,1024]{1,0:T(8,128)(2,1)}, u32[]{:S(2)}) %copy-start.2) | copy-done | bytes 262168
  8.1 0.9 %copy-done.3 = bf16[128,1024]{1,0:T(8,128)(2,1)S(1)} copy-done((bf16[128,1024]{1,0:T(8,128)(2,1)S(1)}, bf16[128,1024]{1,0:T(8,128)(2,1)}, u32[]{:S(2)}) %copy-start.3) | copy-done | bytes 262168
  9.0 1.2 %local_state.1 = (f32[1024,128]{1,0:T(8,128)S(1)}, f32[128,128]{1,0:T(8,128)S(1)}) custom-call(bf16[128,1024]{1,0:T(8,128)(2,1)S(1)} %copy-done.3, bf16[128,1024]{1,0:T(8,128)(2,1)S(1)} %copy-done.2, f32[3,7,1024]{2,1,0:T(8,128)S(1)} %copy-done.1, f32[16,1024]{1,0:T(8,128)S(1)} %copy-done), custom_call_target="tpu_custom_call" | custom-call | tf_op jit(solution)/shard_map/local_state/pallas_call | solution.py:273
  10.2 0.8 %edge_state.1 = (bf16[1024,128]{1,0:T(8,128)(2,1)}, f32[64,128]{1,0:T(8,128)S(1)}) custom-call(bf16[24,1024]{1,0:T(8,128)(2,1)S(1)} %collective-permute-done.halo_ref, bf16[16,1024]{1,0:T(8,128)(2,1)S(1)} %slice.18.k_ref, bf16[16,1024]{1,0:T(8,128)(2,1)S(1)} %slice.19.v_ref, f32[3,7,1024]{2,1,0:T(8,128)S(1)} %copy-done.1, f32[16,1024]{1,0:T(8,128)S(1)} %copy-done, ...), custom_call_target="tpu_custom_call" | custom-call | tf_op jit(solution)/shard_map/edge_state/pallas_call | solution.py:278
  11.0 5.9 %all-to-all-start = ((bf16[8,128,128]{2,1,0:T(8,128)(2,1)}), bf16[8,128,128]{2,1,0:T(8,128)(2,1)S(1)}, u32[]{:S(2)}, u32[]{:S(2)}) async-start(bf16[8,128,128]{2,1,0:T(8,128)(2,1)} %bitcast.2), calls=%async_computation | async-start | bytes 524288 | tf_op jit(solution)/shard_map/all_to_all | solution.py:283
  16.9 0.1 pad_add_fusion.at_ref
  17.0 9.8 %all-to-all-done = bf16[8,128,128]{2,1,0:T(8,128)(2,1)S(1)} async-done(((bf16[8,128,128]{2,1,0:T(8,128)(2,1)}), bf16[8,128,128]{2,1,0:T(8,128)(2,1)S(1)}, u32[]{:S(2)}, u32[]{:S(2)}) %all-to-all-start) | async-done | bytes 262176 | tf_op jit(solution)/shard_map/all_to_all | solution.py:283
  26.8 1.3 %scan_near.1 = (bf16[1024,128]{1,0:T(8,128)(2,1)}, f32[128,128]{1,0:T(8,128)S(1)}) custom-call(s32[2]{0:T(128)S(1)} %pad_add_fusion.at_ref, bf16[1024,128]{1,0:T(8,128)(2,1)S(1)} %bitcast.12, f32[16,1024]{1,0:T(8,128)S(1)} %copy-done), custom_call_target="tpu_custom_call" | custom-call | tf_op jit(solution)/shard_map/scan_near/pallas_call | solution.py:289
  28.1 10.4 %all-to-all-start.1 = ((bf16[8,128,128]{2,1,0:T(8,128)(2,1)}), bf16[8,128,128]{2,1,0:T(8,128)(2,1)S(1)}, u32[]{:S(2)}, u32[]{:S(2)}) async-start(bf16[8,128,128]{2,1,0:T(8,128)(2,1)} %bitcast.4), calls=%async_computation.1 | async-start | bytes 524288 | tf_op jit(solution)/shard_map/all_to_all | solution.py:292
  38.6 0.7 %copy-done.6 = f32[1024]{0:T(1024)S(1)} copy-done((f32[1024]{0:T(1024)S(1)}, f32[1024]{0:T(1024)}, u32[]{:S(2)}) %copy-start.6) | copy-done | bytes 4120
  39.3 1.5 %own_part.1 = (f32[1024,128]{1,0:T(8,128)S(1)}, f32[1024,128]{1,0:T(8,128)S(1)}) custom-call(bf16[24,1024]{1,0:T(8,128)(2,1)S(1)} %collective-permute-done.halo_ref, bf16[128,1024]{1,0:T(8,128)(2,1)S(1)} %copy-done.4, f32[1024,128]{1,0:T(8,128)S(1)} %get-tuple-element.17.u_ref, f32[64,128]{1,0:T(8,128)S(1)} %get-tuple-element.18.edge_ref, ...), custom_call_target="tpu_custom_call" | custom-call | tf_op jit(solution)/shard_map/own_part/pallas_call | solution.py:284
  40.8 7.1 %all-to-all-done.1 = bf16[8,128,128]{2,1,0:T(8,128)(2,1)S(1)} async-done(((bf16[8,128,128]{2,1,0:T(8,128)(2,1)}), bf16[8,128,128]{2,1,0:T(8,128)(2,1)S(1)}, u32[]{:S(2)}, u32[]{:S(2)}) %all-to-all-start.1) | async-done | bytes 262176 | tf_op jit(solution)/shard_map/all_to_all | solution.py:292
  48.0 0.7 %copy-done.7 = f32[1024]{0:T(1024)S(1)} copy-done((f32[1024]{0:T(1024)S(1)}, f32[1024]{0:T(1024)}, u32[]{:S(2)}) %copy-start.7) | copy-done | bytes 4120
  48.7 2.1 %finish.1 = (bf16[128,1024]{1,0:T(8,128)(2,1)}, f32[128,1024]{1,0:T(8,128)S(1)}, f32[8,128]{1,0:T(8,128)S(1)}) custom-call(s32[2]{0:T(128)S(1)} %pad_add_fusion.at_ref, bf16[1024,128]{1,0:T(8,128)(2,1)S(1)} %bitcast.13, f32[128,128]{1,0:T(8,128)S(1)} %get-tuple-element.16.before_ref, f32[16,1024]{1,0:T(8,128)S(1)} %copy-done, ...), custom_call_target="tpu_custom_call" | custom-call | tf_op jit(solution)/shard_map/finish/pallas_call | solution.py:293
  50.8 12.7 %all_to_all.33 = f32[8,1,128]{2,1,0:T(1,128)S(1)} all-to-all(f32[8,1,128]{2,1,0:T(1,128)S(1)} %bitcast.17), channel_id=1, replica_groups=mesh['z'=8,'y'=8,'tensor'=8] {'tensor'}, dimensions={0} | all-to-all | bytes 8192 | tf_op jit(solution)/shard_map/all_to_all | solution.py:299
  63.5 1.0 %normalise.1 = bf16[128,1024]{1,0:T(8,128)(2,1)} custom-call(f32[128,1024]{1,0:T(8,128)S(1)} %get-tuple-element.22.scaled_ref, f32[8,128]{1,0:T(8,128)S(1)} %bitcast.14), custom_call_target="tpu_custom_call" | custom-call | tf_op jit(solution)/shard_map/normalise/pallas_call | solution.py:300
  (18 shorter events, 0.1 us)
Async XLA Ops:
  0.6 0.7 %slice-start.2 = ((bf16[128,1024]{1,0:T(8,128)(2,1)}), bf16[8,1024]{1,0:T(8,128)(2,1)S(1)}, s32[]{:S(2)}) async-start(bf16[128,1024]{1,0:T(8,128)(2,1)} %q_ref.1), calls=%async_computation.5 | async-start | bytes 32768 | tf_op jit(solution)/shard_map/slice | solution.py:270
  0.6 0.7 %slice-start = ((bf16[128,1024]{1,0:T(8,128)(2,1)}), bf16[8,1024]{1,0:T(8,128)(2,1)S(1)}, s32[]{:S(2)}) async-start(bf16[128,1024]{1,0:T(8,128)(2,1)} %v_ref.1), calls=%async_computation.3 | async-start | bytes 32768 | tf_op jit(solution)/shard_map/slice | solution.py:270
  0.7 0.7 %slice-start.1 = ((bf16[128,1024]{1,0:T(8,128)(2,1)}), bf16[8,1024]{1,0:T(8,128)(2,1)S(1)}, s32[]{:S(2)}) async-start(bf16[128,1024]{1,0:T(8,128)(2,1)} %k_ref.1), calls=%async_computation.4 | async-start | bytes 32768 | tf_op jit(solution)/shard_map/slice | solution.py:270
  1.4 5.7 %copy-start.1 = (f32[3,7,1024]{2,1,0:T(8,128)S(1)}, f32[3,7,1024]{2,1,0:T(8,128)}, u32[]{:S(2)}) copy-start(f32[3,7,1024]{2,1,0:T(8,128)} %f_ref.5) | copy-start | bytes 258052
  1.4 5.7 %copy-start = (f32[16,1024]{1,0:T(8,128)S(1)}, f32[16,1024]{1,0:T(8,128)}, u32[]{:S(2)}) copy-start(f32[16,1024]{1,0:T(8,128)} %d_ref.9) | copy-start | bytes 196612
  1.4 8.8 %collective-permute-start = (bf16[24,1024]{1,0:T(8,128)(2,1)S(1)}, bf16[24,1024]{1,0:T(8,128)(2,1)S(1)}, u32[]{:S(2)}, u32[]{:S(2)}) collective-permute-start(bf16[24,1024]{1,0:T(8,128)(2,1)S(1)} %pad_maximum_fusion), channel_id=1, source_target_pairs={{0,8},{8,16},{16,24},{24,32},{32,40},{40,48},{48,56},{56,64},{64,7... | collective-permute-start | bytes 147464 | tf_op jit(solution)/shard_map/ppermute | solution.py:271
  7.1 1.0 %copy-start.2 = (bf16[128,1024]{1,0:T(8,128)(2,1)S(1)}, bf16[128,1024]{1,0:T(8,128)(2,1)}, u32[]{:S(2)}) copy-start(bf16[128,1024]{1,0:T(8,128)(2,1)} %v_ref.1) | copy-start | bytes 786436
  8.0 0.9 %copy-start.3 = (bf16[128,1024]{1,0:T(8,128)(2,1)S(1)}, bf16[128,1024]{1,0:T(8,128)(2,1)}, u32[]{:S(2)}) copy-start(bf16[128,1024]{1,0:T(8,128)(2,1)} %k_ref.1) | copy-start | bytes 786436
  11.0 15.8 %all-to-all-start = ((bf16[8,128,128]{2,1,0:T(8,128)(2,1)}), bf16[8,128,128]{2,1,0:T(8,128)(2,1)S(1)}, u32[]{:S(2)}, u32[]{:S(2)}) async-start(bf16[8,128,128]{2,1,0:T(8,128)(2,1)} %bitcast.2), calls=%async_computation | async-start | bytes 524288 | tf_op jit(solution)/shard_map/all_to_all | solution.py:283
  28.1 10.4 %copy-start.8 = (f32[16,1024]{1,0:T(8,128)S(1)}, f32[16,1024]{1,0:T(8,128)}, u32[]{:S(2)}) copy-start(f32[16,1024]{1,0:T(8,128)} %param.13) | copy-start | bytes 196612
  28.1 10.5 %copy-start.4 = (bf16[128,1024]{1,0:T(8,128)(2,1)S(1)}, bf16[128,1024]{1,0:T(8,128)(2,1)}, u32[]{:S(2)}) copy-start(bf16[128,1024]{1,0:T(8,128)(2,1)} %q_ref.1) | copy-start | bytes 786436
  28.1 19.8 %all-to-all-start.1 = ((bf16[8,128,128]{2,1,0:T(8,128)(2,1)}), bf16[8,128,128]{2,1,0:T(8,128)(2,1)S(1)}, u32[]{:S(2)}, u32[]{:S(2)}) async-start(bf16[8,128,128]{2,1,0:T(8,128)(2,1)} %bitcast.4), calls=%async_computation.1 | async-start | bytes 524288 | tf_op jit(solution)/shard_map/all_to_all | solution.py:292
  38.6 0.7 %copy-start.6 = (f32[1024]{0:T(1024)S(1)}, f32[1024]{0:T(1024)}, u32[]{:S(2)}) copy-start(f32[1024]{0:T(1024)} %param.15) | copy-start | bytes 12292
  39.3 8.7 %copy-start.5 = (bf16[128,1024]{1,0:T(8,128)(2,1)S(1)}, bf16[128,1024]{1,0:T(8,128)(2,1)}, u32[]{:S(2)}) copy-start(bf16[128,1024]{1,0:T(8,128)(2,1)} %residual_ref.1) | copy-start | bytes 786436
  48.0 0.7 %copy-start.7 = (f32[1024]{0:T(1024)S(1)}, f32[1024]{0:T(1024)}, u32[]{:S(2)}) copy-start(f32[1024]{0:T(1024)} %param.17) | copy-start | bytes 12292
where the time goes:
time: 65.2 us; the launch traced here: 64.5 us
  starting transfers between devices  20.5 us (31%)
  waiting for transfers between devices  16.9 us (26%)
  blocking collectives  12.7 us (19%)
  Pallas kernels  8.03 us (12%)
  local copies, waits for them, and re-layouts  5.52 us (8%)
  between operations  0.73 us (1%)
    all_to_all x1, blocking collectives, shards(): gathered = lax.all_to_all(squares, 'tensor', 0, 0, tiled=True)  12.7 us
    all_to_all x1, starting transfers between devices, shards(): far = lax.all_to_all(totals, 'z', 0, 0, tiled=True)  10.4 us
    all_to_all x1, waiting for transfers between devices, shards(): near = lax.all_to_all(sent, 'y', 0, 0, tiled=True)  9.76 us
    all_to_all x1, waiting for transfers between devices, shards(): far = lax.all_to_all(totals, 'z', 0, 0, tiled=True)  7.13 us
    all_to_all x1, starting transfers between devices, shards(): near = lax.all_to_all(sent, 'y', 0, 0, tiled=True)  5.92 us
    ppermute x1, starting transfers between devices, shards(): halo = lax.ppermute(tails, ('z', 'y'), [(i, i + 1) for i in range(63)])  4.16 us
    unnamed x18, local copies, waits for them, and re-layouts  3.27 us
    pallas_call x1, Pallas kernels, shards(): call(finish, 'finish', [((ROWS, 1024), bf16), ((ROWS, 1024), f32), ((8, L...  2.14 us
  transfers between devices with their start and end apart: 3, of which 2 were waited for; matrix products, arithmetic and copies ran while one was open for 3% of the time, Pallas kernels for 4%

commit v1 on v0

v1 whole, which is shorter than its diff:
```python
import jax
import jax.numpy as jnp
from jax import lax
from jax.experimental import pallas as pl
from jax.experimental.pallas import tpu as pltpu
from jax.sharding import Mesh, PartitionSpec as P

D = 8192
ORDER = 16
TAPS = 7
ROWS = 128
LANES = 128
GROUPS = 8
LIMIT = 54300 << 10
BLOCK = 8

f32 = jnp.float32
bf16 = jnp.bfloat16


def stack_rows(dst, src, first, rows, at, step=16):
    for r in range(0, rows, step):
        for j in range(GROUPS):
            tile = src[first + r : first + r + step, j * LANES : (j + 1) * LANES]
            dst[pl.ds((at + r) * GROUPS + j, step, stride=GROUPS), :] = tile.astype(f32)


def stack_taps(dst, taps, which):
    for j in range(GROUPS):
        dst[pl.ds(j, TAPS, stride=GROUPS), :] = taps[which, :, j * LANES : (j + 1) * LANES]


def row(ref, n):
    return ref[pl.ds(pl.multiple_of(n * GROUPS, GROUPS), GROUPS), :]


def put(ref, n, value):
    ref[pl.ds(pl.multiple_of(n * GROUPS, GROUPS), GROUPS), :] = value


def conv(ref, taps, n0, count):
    rows = [row(ref, n0 + 8 - (TAPS - 1) + i) for i in range(count + TAPS - 1)]
    out = []
    for i in range(count):
        total = rows[i + TAPS - 1] * taps[0]
        for j in range(1, TAPS):
            total = total + rows[i + TAPS - 1 - j] * taps[j]
        out.append(total)
    return out


def rows_of(ref, count):
    return [row(ref, m) for m in range(count)]


def total_of(values):
    values = list(values)
    while len(values) > 1:
        values = [a + b for a, b in zip(values[::2], values[1::2])] + (
            [values[-1]] if len(values) % 2 else []
        )
    return values[0]


def call(body, name, outs, scratch, count, scalars=0, far=(), limit=32 << 20, far_out=False):
    spec = pl.BlockSpec(memory_space=pltpu.VMEM)
    kinds = {i: pl.BlockSpec(memory_space=pltpu.SMEM) for i in range(scalars)}
    kinds.update({i: pl.BlockSpec(memory_space=pltpu.HBM) for i in far})
    return pl.pallas_call(
        body,
        name=name,
        out_shape=tuple(jax.ShapeDtypeStruct(s, t) for s, t in outs),
        in_specs=[kinds.get(i, spec) for i in range(count)],
        out_specs=tuple(pl.BlockSpec(memory_space=pltpu.HBM) if far_out else spec for _ in outs),
        scratch_shapes=scratch,
        compiler_params=pltpu.CompilerParams(vmem_limit_bytes=limit),
    )


def fetch(q_hbm, k_hbm, v_hbm, tails, q_out, k_out, v_out, sems):
    copies = []
    for i, (src, dst) in enumerate(((q_hbm, q_out), (k_hbm, k_out), (v_hbm, v_out))):
        ends = src.at[pl.ds(ROWS - 8, 8)], tails.at[pl.ds(8 * i, 8)]
        copies.append(pltpu.make_async_copy(*ends, sems.at[0, i]))
        copies.append(pltpu.make_async_copy(src, dst, sems.at[1, i]))
    for copy in copies[::2] + copies[1::2]:
        copy.start()
    for copy in copies:
        copy.wait()


def one_less_exp(d):
    square = d * d
    series = 1.0 + square / 72.0
    for divisor in (42.0, 20.0, 6.0):
        series = 1.0 + square * (1.0 / divisor) * series
    return 2.0 * jnp.exp(-d) * d * series


def local_part(
    at_ref, q_ref, k_ref, v_ref, f_ref, d_ref, r_ref, skip_ref, gain_ref,
    qc_ref, g_ref, state_ref, taps_ref, heads_ref, dt, wt, st, gain_out, qt, kt, vt, rt,
):
    del at_ref
    gain_out[...] = gain_ref[...]
    for i, (src, dst) in enumerate(((q_ref, qt), (k_ref, kt), (v_ref, vt))):
        stack_taps(taps_ref.at[pl.ds(8 * GROUPS * i, 8 * GROUPS)], f_ref, i)
        stack_rows(dst, src, 0, ROWS, 8)
        heads_ref[8 * GROUPS * i : 8 * GROUPS * (i + 1), :] = dst[8 * GROUPS : 16 * GROUPS, :]
    stack_rows(dt, d_ref, 0, ORDER, 0)
    stack_rows(rt, r_ref, 0, ORDER, 0)
    wt[...] = rt[...] * jnp.sqrt(one_less_exp(dt[...]))
    for j in range(GROUPS):
        st[j : j + 1, :] = skip_ref[0:1, j * LANES : (j + 1) * LANES]
    taps = [[row(taps_ref, 8 * i + j) for j in range(TAPS)] for i in range(3)]
    pole = [jnp.exp(-d) for d in rows_of(dt, ORDER)]
    skip = st[...]

    def block(n0, count, state):
        for i, c in enumerate(conv(qt, taps[0], n0, count)):
            put(qc_ref, n0 + i, c)
        us = [a * b for a, b in zip(conv(kt, taps[1], n0, count), conv(vt, taps[2], n0, count))]
        for i, u in enumerate(us):
            state = [u] * ORDER if state is None else [p * s + u for p, s in zip(pole, state)]
            terms = [row(wt, m) * s for m, s in enumerate(state)]
            put(g_ref, n0 + i, total_of(terms + [skip * u]))
        return state

    edge = TAPS - 1
    state = block(edge, BLOCK - edge, None)
    state = lax.fori_loop(
        1, ROWS // BLOCK, lambda b, s: tuple(block(b * BLOCK, BLOCK, list(s))), tuple(state)
    )
    for m in range(ORDER):
        put(state_ref, m, state[m])


def edge_part(halo_ref, heads_ref, taps_ref, dt, state_ref, out_ref, edge_ref, xt):
    edge = TAPS - 1
    convs = []
    for i in range(3):
        at = xt.at[pl.ds(16 * GROUPS * i, 16 * GROUPS)]
        stack_rows(at, halo_ref, 8 * i, 8, 0, 8)
        at[8 * GROUPS : 16 * GROUPS, :] = heads_ref[8 * GROUPS * i : 8 * GROUPS * (i + 1), :]
        convs.append(conv(at, [row(taps_ref, 8 * i + j) for j in range(TAPS)], 0, edge))
    us = [a * b for a, b in zip(convs[1], convs[2])]
    for i in range(edge):
        put(edge_ref, i, us[i])
        put(edge_ref, 8 + i, convs[0][i])
    for m in range(0, ORDER, 2):
        pair = []
        for i in (m, m + 1):
            d = row(dt, i)
            p = jnp.exp(-d)
            s = us[0]
            for u in us[1:]:
                s = p * s + u
            pair.append(row(state_ref, i) + jnp.exp(-(ROWS - edge) * d) * s)
        both = jnp.concatenate(pair, axis=0).astype(bf16)
        for copy in range(8):
            out_ref[(copy * ORDER + m) * GROUPS : (copy * ORDER + m + 2) * GROUPS, :] = both


def load_pair(ref, block, m):
    both = ref[(block * ORDER + m) * GROUPS : (block * ORDER + m + 2) * GROUPS, :].astype(f32)
    return both[:GROUPS], both[GROUPS:]


def scan_blocks(ref, m, steps, index):
    zero = jnp.zeros((GROUPS, LANES), f32)
    total, before = [zero, zero], [zero, zero]
    for b in range(8):
        here = index == b
        before = [jnp.where(here, t, o) for t, o in zip(total, before)]
        total = [s * t + x for s, t, x in zip(steps, total, load_pair(ref, b, m))]
    return before, total


def scan_near(at_ref, got_ref, dt, out_ref, before_ref):
    index = at_ref[1]
    for m in range(0, ORDER, 2):
        steps = [jnp.exp(-float(ROWS) * row(dt, i)) for i in (m, m + 1)]
        before, total = scan_blocks(got_ref, m, steps, index)
        for i in range(2):
            put(before_ref, m + i, before[i])
        both = jnp.concatenate(total, axis=0).astype(bf16)
        for copy in range(8):
            out_ref[(copy * ORDER + m) * GROUPS : (copy * ORDER + m + 2) * GROUPS, :] = both


def finish(
    at_ref, got_ref, before_ref, dt, wt, skip_ref, qc_ref, g_ref, edge_ref, residual_ref, gain_ref,
    mixed_ref, scaled_ref, squares_ref, st, mt, sq,
):
    far, near = at_ref[0], at_ref[1].astype(f32)
    for m in range(0, ORDER, 2):
        rates = [row(dt, i) for i in (m, m + 1)]
        steps = [jnp.exp(-float(8 * ROWS) * d) for d in rates]
        before, _ = scan_blocks(got_ref, m, steps, far)
        for i in range(2):
            entry = row(before_ref, m + i) + jnp.exp(-float(ROWS) * near * rates[i]) * before[i]
            put(st, m + i, row(wt, m + i) * entry)
    pole = [jnp.exp(-d) for d in rows_of(dt, ORDER)]
    skip = skip_ref[...]
    count = 16

    def block(n0, state, edge):
        state = list(state)
        for i in range(count):
            state = [p * s for p, s in zip(pole, state)]
            if i < edge:
                u = row(edge_ref, i)
                state = [s + row(wt, m) * u for m, s in enumerate(state)]
                value = row(edge_ref, 8 + i) * (skip * u + total_of(state))
            else:
                value = row(qc_ref, n0 + i) * (row(g_ref, n0 + i) + total_of(state))
            mt[i * GROUPS : (i + 1) * GROUPS, :] = value
        at = pl.ds(pl.multiple_of(n0, count), count)
        squares = None
        for j in range(GROUPS):
            lanes = slice(j * LANES, (j + 1) * LANES)
            tile = mt[pl.ds(j, count, stride=GROUPS), :].astype(bf16)
            mixed_ref[at, lanes] = tile
            summed = residual_ref[at, lanes].astype(f32) + tile.astype(f32)
            scaled_ref[at, lanes] = summed * gain_ref[0:1, lanes]
            part = summed * summed
            squares = part if squares is None else squares + part
        sq[at, :] = squares
        return tuple(state)

    state = block(0, rows_of(st, ORDER), TAPS - 1)
    lax.fori_loop(1, ROWS // count, lambda b, s: block(b * count, s, 0), state)
    squares_ref[...] = lax.dot_general(
        jnp.ones((8, LANES), f32), sq[...], (((1,), (1,)), ((), ())),
        precision=lax.Precision.HIGHEST, preferred_element_type=f32,
    )


def normalise(mixed_ref, scaled_ref, squares_ref, mixed_hbm, out_hbm, out, sems):
    first = pltpu.make_async_copy(mixed_ref, mixed_hbm, sems.at[0])
    first.start()
    total = lax.dot_general(
        squares_ref[...], jnp.ones((8, LANES), f32), (((0,), (0,)), ((), ())),
        precision=lax.Precision.HIGHEST, preferred_element_type=f32,
    )
    factor = lax.rsqrt(total / D + 1e-05)
    half = ROWS // 2
    copies = [first]
    for part in range(2):
        rows = slice(part * half, (part + 1) * half)
        for j in range(GROUPS):
            lanes = slice(j * LANES, (j + 1) * LANES)
            out[rows, lanes] = (scaled_ref[rows, lanes] * factor[rows]).astype(bf16)
        at = pl.ds(part * half, half)
        copy = pltpu.make_async_copy(out.at[at], out_hbm.at[at], sems.at[1 + part])
        copy.start()
        copies.append(copy)
    for copy in copies:
        copy.wait()


def shards(query, key, value, short_filter, residues, decay, skip_gain, residual, norm_gain):
    stacked = ((ROWS + 8) * GROUPS, LANES)
    modes = (ORDER * GROUPS, LANES)
    taps = (24 * GROUPS, LANES)
    blocks = (8 * ORDER * GROUPS, LANES)
    whole = (ROWS * GROUPS, LANES)
    natural = (ROWS, query.shape[1])
    vmem = pltpu.VMEM

    at = jnp.stack([lax.axis_index("z"), lax.axis_index("y")]).astype(jnp.int32)
    tails, q_here, k_here, v_here = call(
        fetch, "fetch", [((24, natural[1]), bf16)] + [(natural, bf16)] * 3, [pltpu.SemaphoreType.DMA((2, 3))],
        3, far=(0, 1, 2), limit=LIMIT,
    )(query, key, value)
    halo = lax.ppermute(tails, ("z", "y"), [(i, i + 1) for i in range(63)])
    qc, own, clean, taps_t, heads, rates, weights, skip, gain = call(
        local_part, "local_part",
        [(whole, f32)] * 2 + [(modes, f32)] + [(taps, f32)] * 2 + [(modes, f32)] * 2
        + [((GROUPS, LANES), f32), ((1, natural[1]), f32)],
        [vmem(stacked, f32)] * 3 + [vmem(modes, f32)], 9, 1,
    )(at, q_here, k_here, v_here, short_filter, decay, residues, skip_gain[None], norm_gain[None])
    sent, edge = call(
        edge_part, "edge_part", [(blocks, bf16), ((16 * GROUPS, LANES), f32)], [vmem((48 * GROUPS, LANES), f32)], 5,
    )(halo, heads, taps_t, rates, clean)
    near = lax.all_to_all(sent, "y", 0, 0, tiled=True)
    totals, before = call(
        scan_near, "scan_near", [(blocks, bf16), (modes, f32)], [], 3, 1,
    )(at, near, rates)
    far = lax.all_to_all(totals, "z", 0, 0, tiled=True)
    mixed, scaled, squares = call(
        finish, "finish",
        [(natural, bf16), (natural, f32), ((8, LANES), f32)],
        [vmem(modes, f32), vmem((16 * GROUPS, LANES), f32), vmem((ROWS, LANES), f32)],
        11, 1,
    )(at, far, before, rates, weights, skip, qc, own, edge, residual, gain)
    gathered = lax.all_to_all(squares, "tensor", 0, 0, tiled=True)
    return call(
        normalise, "normalise", [(natural, bf16)] * 2, [vmem(natural, bf16), pltpu.SemaphoreType.DMA((3,))],
        3, far_out=True,
    )(mixed, scaled, gathered)


def solution(mesh):
    context = ("z", "y")
    split = Mesh(mesh.devices.reshape(8, 8, 8), ("z", "y", "tensor"))
    rows = P(context, "tensor")
    in_specs = (
        rows, rows, rows, P(None, None, "tensor"), P(None, "tensor"), P(None, "tensor"),
        P("tensor"), rows, P("tensor"),
    )
    return jax.shard_map(shards, mesh=split, in_specs=in_specs, out_specs=(rows, rows), check_vma=False)
```

time: 65.2 us -> 61.4 us (0.942)
  blocking collectives: 12.7 us -> 48.1 us
  waiting for transfers between devices: 16.9 us -> 0.01 us
  starting transfers between devices: 20.5 us -> 4.03 us
  local copies, waits for them, and re-layouts: 5.52 us -> 0.7 us
    all_to_all x0 -> x2, blocking collectives: none -> 34.6 us  [the longest x1 19.4 us: shards(): far = lax.all_to_all(totals, 'z', 0, 0, tiled=True)]
    all_to_all x2 -> x0, waiting for transfers between devices: 16.9 us -> none  [the longest x1 9.76 us: shards(): near = lax.all_to_all(sent, 'y', 0, 0, tiled=True)]
    all_to_all x2 -> x0, starting transfers between devices: 16.3 us -> none  [the longest x1 10.4 us: shards(): far = lax.all_to_all(totals, 'z', 0, 0, tiled=True)]
    unnamed x18 -> x12, local copies, waits for them, and re-layouts: 3.27 us -> 0.7 us
    slice x8 -> x0, local copies, waits for them, and re-layouts: 2.25 us -> none  [the longest x1 0.76 us: shards(): key[:16]]
    all_to_all x1, blocking collectives: 12.7 us -> 13.6 us  [shards(): gathered = lax.all_to_all(squares, 'tensor', 0, 0, tiled=True)]
  transfers between devices with their start and end apart: 3 -> 1, of which waited for: 2 -> 0; matrix products, arithmetic and copies ran while one was open for 3% -> 0% of each run, Pallas kernels for 4% -> 5%
where the time goes in v1:
time: 61.4 us; the launch traced here: 61.1 us
  blocking collectives  48.1 us (78%)
  Pallas kernels  7.41 us (12%)
  starting transfers between devices  4.03 us (7%)
  between operations  0.72 us (1%)
  local copies, waits for them, and re-layouts  0.7 us (1%)
    all_to_all x1, blocking collectives, shards(): far = lax.all_to_all(totals, 'z', 0, 0, tiled=True)  19.4 us
    all_to_all x1, blocking collectives, shards(): near = lax.all_to_all(sent, 'y', 0, 0, tiled=True)  15.1 us
    all_to_all x1, blocking collectives, shards(): gathered = lax.all_to_all(squares, 'tensor', 0, 0, tiled=True)  13.6 us
    ppermute x1, starting transfers between devices, shards(): halo = lax.ppermute(tails, ('z', 'y'), [(i, i + 1) for i in range(63)])  4.03 us
    pallas_call x1, Pallas kernels, shards(): call(local_part, 'local_part', [(whole, f32)] * 2 + [(modes, f32)] + [(ta...  2.77 us
    pallas_call x1, Pallas kernels, shards(): call(finish, 'finish', [(natural, bf16), (natural, f32), ((8, LANES), f32...  1.65 us
    pallas_call x1, Pallas kernels, shards(): call(fetch, 'fetch', [((24, natural[1]), bf16)] + [(natural, bf16)] * 3,...  1.26 us
  transfers between devices with their start and end apart: 1, of which 0 were waited for; matrix products, arithmetic and copies ran while one was open for 0% of the time, Pallas kernels for 5%

profile of v1, /device:TPU:1, one launch (start us, length us, event | category | flops | bytes accessed | tf_op | source)
XLA Modules:
  0.0 61.1 jit_solution(12274474513225578480)
XLA Ops:
  0.6 0.0 copy-start.1
  0.6 0.0 copy-start.2
  0.7 0.0 copy-start.3
  0.7 1.3 %fetch.1 = (bf16[24,1024]{1,0:T(8,128)(2,1)S(1)}, bf16[128,1024]{1,0:T(8,128)(2,1)S(1)}, bf16[128,1024]{1,0:T(8,128)(2,1)S(1)}, bf16[128,1024]{1,0:T(8,128)(2,1)S(1)}) custom-call(bf16[128,1024]{1,0:T(8,128)(2,1)} %q_hbm.1, bf16[128,1024]{1,0:T(8,128)(2,1)} %k_hbm.1, bf16[128,1024]{1,0:T(8,128)(2,1)} %v_hbm.1), custom_call_target="tpu_custom_call" | custom-call | tf_op jit(solution)/shard_map/fetch/pallas_call | solution.py:272
  1.9 4.0 %collective-permute-start = (bf16[24,1024]{1,0:T(8,128)(2,1)S(1)}, bf16[24,1024]{1,0:T(8,128)(2,1)S(1)}, u32[]{:S(2)}, u32[]{:S(2)}) collective-permute-start(bf16[24,1024]{1,0:T(8,128)(2,1)S(1)} %get-tuple-element.22), channel_id=1, source_target_pairs={{0,8},{8,16},{16,24},{24,32},{32,40},{40,48},{48,56},{56,64},{64,7... | collective-permute-start | bytes 147464 | tf_op jit(solution)/shard_map/ppermute | solution.py:276
  6.0 0.1 pad_add_fusion.at_ref
  6.0 0.0 copy-start.5
  6.0 0.0 copy-start.4
  6.0 0.0 copy-done.1
  6.1 0.0 copy-done.2
  6.1 0.0 copy-done.3
  6.1 0.7 %copy-done.5 = f32[1024]{0:T(1024)S(1)} copy-done((f32[1024]{0:T(1024)S(1)}, f32[1024]{0:T(1024)}, u32[]{:S(2)}) %copy-start.5) | copy-done | bytes 4120
  6.7 0.0 copy-done.4
  6.7 2.8 %local_part.1 = (f32[1024,128]{1,0:T(8,128)S(1)}, f32[1024,128]{1,0:T(8,128)S(1)}, f32[128,128]{1,0:T(8,128)S(1)}, f32[192,128]{1,0:T(8,128)S(1)}, f32[192,128]{...) custom-call(s32[2]{0:T(128)S(1)} %pad_add_fusion.at_ref, ...), custom_call_target="tpu_custom_call" | custom-call | tf_op jit(solution)/shard_map/local_part/pallas_call | solution.py:277
  9.5 0.0 collective-permute-done.halo_ref
  9.5 0.1 edge_part.1
  9.6 15.1 %all_to_all.33 = bf16[8,128,128]{2,1,0:T(8,128)(2,1)S(1)} all-to-all(bf16[8,128,128]{2,1,0:T(8,128)(2,1)S(1)} %bitcast.14), channel_id=1, replica_groups=mesh['z'=8,'y'=8,'tensor'=8] {'y'}, dimensions={0} | all-to-all | bytes 524288 | tf_op jit(solution)/shard_map/all_to_all | solution.py:286
  24.8 0.6 %scan_near.1 = (bf16[1024,128]{1,0:T(8,128)(2,1)S(1)}, f32[128,128]{1,0:T(8,128)S(1)}) custom-call(s32[2]{0:T(128)S(1)} %pad_add_fusion.at_ref, bf16[1024,128]{1,0:T(8,128)(2,1)S(1)} %bitcast.12, f32[128,128]{1,0:T(8,128)S(1)} %get-tuple-element.28.dt), custom_call_target="tpu_custom_call" | custom-call | tf_op jit(solution)/shard_map/scan_near/pallas_call | solution.py:287
  25.4 0.0 copy-start
  25.4 19.4 %all_to_all.34 = bf16[8,128,128]{2,1,0:T(8,128)(2,1)S(1)} all-to-all(bf16[8,128,128]{2,1,0:T(8,128)(2,1)S(1)} %bitcast.15), channel_id=1, replica_groups=mesh['z'=8,'y'=8,'tensor'=8] {'z'}, dimensions={0} | all-to-all | bytes 524288 | tf_op jit(solution)/shard_map/all_to_all | solution.py:290
  44.8 0.0 copy-done
  44.8 1.6 %finish.1 = (bf16[128,1024]{1,0:T(8,128)(2,1)S(1)}, f32[128,1024]{1,0:T(8,128)S(1)}, f32[8,128]{1,0:T(8,128)S(1)}) custom-call(s32[2]{0:T(128)S(1)} %pad_add_fusion.at_ref, bf16[1024,128]{1,0:T(8,128)(2,1)S(1)} %bitcast.13, f32[128,128]{1,0:T(8,128)S(1)} %get-tuple-element.32.before_ref, f32[128,128]{1,0:T(8,128)S(1)} %get-tuple-element.28.dt, ...), custom_call_target="tpu_custom_call" | custom-call | tf_op jit(solution)/shard_map/finish/pallas_call | solution.py:291
  46.5 13.6 %all_to_all.35 = f32[8,1,128]{2,1,0:T(1,128)S(1)} all-to-all(f32[8,1,128]{2,1,0:T(1,128)S(1)} %bitcast.19), channel_id=1, replica_groups=mesh['z'=8,'y'=8,'tensor'=8] {'tensor'}, dimensions={0} | all-to-all | bytes 8192 | tf_op jit(solution)/shard_map/all_to_all | solution.py:297
  60.1 1.0 %normalise.1 = (bf16[128,1024]{1,0:T(8,128)(2,1)}, bf16[128,1024]{1,0:T(8,128)(2,1)}) custom-call(bf16[128,1024]{1,0:T(8,128)(2,1)S(1)} %get-tuple-element.39.mixed_ref, f32[128,1024]{1,0:T(8,128)S(1)} %get-tuple-element.40.scaled_ref, f32[8,128]{1,0:T(8,128)S(1)} %bitcast.16), custom_call_target="tpu_custom_call" | custom-call | tf_op jit(solution)/shard_map/normalise/pallas_call | solution.py:298
Async XLA Ops:
  0.6 5.4 %copy-start.1 = (f32[3,7,1024]{2,1,0:T(8,128)S(1)}, f32[3,7,1024]{2,1,0:T(8,128)}, u32[]{:S(2)}) copy-start(f32[3,7,1024]{2,1,0:T(8,128)} %f_ref.1) | copy-start | bytes 258052
  0.6 5.4 %copy-start.2 = (f32[16,1024]{1,0:T(8,128)S(1)}, f32[16,1024]{1,0:T(8,128)}, u32[]{:S(2)}) copy-start(f32[16,1024]{1,0:T(8,128)} %d_ref.1) | copy-start | bytes 196612
  0.7 5.4 %copy-start.3 = (f32[16,1024]{1,0:T(8,128)S(1)}, f32[16,1024]{1,0:T(8,128)}, u32[]{:S(2)}) copy-start(f32[16,1024]{1,0:T(8,128)} %r_ref.1) | copy-start | bytes 196612
  1.9 7.6 %collective-permute-start = (bf16[24,1024]{1,0:T(8,128)(2,1)S(1)}, bf16[24,1024]{1,0:T(8,128)(2,1)S(1)}, u32[]{:S(2)}, u32[]{:S(2)}) collective-permute-start(bf16[24,1024]{1,0:T(8,128)(2,1)S(1)} %get-tuple-element.22), channel_id=1, source_target_pairs={{0,8},{8,16},{16,24},{24,32},{32,40},{40,48},{48,56},{56,64},{64,7... | collective-permute-start | bytes 147464 | tf_op jit(solution)/shard_map/ppermute | solution.py:276
  6.0 0.7 %copy-start.5 = (f32[1024]{0:T(1024)S(1)}, f32[1024]{0:T(1024)}, u32[]{:S(2)}) copy-start(f32[1024]{0:T(1024)} %param.17) | copy-start | bytes 12292
  6.0 0.7 %copy-start.4 = (f32[1024]{0:T(1024)S(1)}, f32[1024]{0:T(1024)}, u32[]{:S(2)}) copy-start(f32[1024]{0:T(1024)} %param.15) | copy-start | bytes 12292
  25.4 19.5 %copy-start = (bf16[128,1024]{1,0:T(8,128)(2,1)S(1)}, bf16[128,1024]{1,0:T(8,128)(2,1)}, u32[]{:S(2)}) copy-start(bf16[128,1024]{1,0:T(8,128)(2,1)} %residual_ref.1) | copy-start | bytes 786436

commit v2 on v1

--- a/solution.py
+++ b/solution.py
@@ -12,6 +12,7 @@
 LANES = 128
 GROUPS = 8
 LIMIT = 54300 << 10
+CONTEXT = ("half", "place", "y")
 BLOCK = 8
 
 f32 = jnp.float32
@@ -166,39 +167,48 @@
     return both[:GROUPS], both[GROUPS:]
 
 
-def scan_blocks(ref, m, steps, index):
-    zero = jnp.zeros((GROUPS, LANES), f32)
-    total, before = [zero, zero], [zero, zero]
-    for b in range(8):
-        here = index == b
-        before = [jnp.where(here, t, o) for t, o in zip(total, before)]
+def scan_blocks(ref, m, steps, count, index=None):
+    total = load_pair(ref, 0, m)
+    before = [jnp.zeros_like(total[0])] * 2
+    for b in range(1, count):
+        if index is not None:
+            before = [jnp.where(index == b, t, o) for t, o in zip(total, before)]
         total = [s * t + x for s, t, x in zip(steps, total, load_pair(ref, b, m))]
     return before, total
 
 
 def scan_near(at_ref, got_ref, dt, out_ref, before_ref):
-    index = at_ref[1]
+    index = at_ref[2]
     for m in range(0, ORDER, 2):
         steps = [jnp.exp(-float(ROWS) * row(dt, i)) for i in (m, m + 1)]
-        before, total = scan_blocks(got_ref, m, steps, index)
+        before, total = scan_blocks(got_ref, m, steps, 8, index)
         for i in range(2):
             put(before_ref, m + i, before[i])
         both = jnp.concatenate(total, axis=0).astype(bf16)
-        for copy in range(8):
+        for copy in range(4):
             out_ref[(copy * ORDER + m) * GROUPS : (copy * ORDER + m + 2) * GROUPS, :] = both
 
 
+def sum_half(got_ref, dt, out_ref):
+    for m in range(0, ORDER, 2):
+        steps = [jnp.exp(-float(8 * ROWS) * row(dt, i)) for i in (m, m + 1)]
+        _, total = scan_blocks(got_ref, m, steps, 4)
+        out_ref[m * GROUPS : (m + 2) * GROUPS, :] = jnp.concatenate(total, axis=0).astype(bf16)
+
+
 def finish(
-    at_ref, got_ref, before_ref, dt, wt, skip_ref, qc_ref, g_ref, edge_ref, residual_ref, gain_ref,
+    at_ref, got_ref, half_ref, before_ref, dt, wt, skip_ref, qc_ref, g_ref, edge_ref, residual_ref, gain_ref,
     mixed_ref, scaled_ref, squares_ref, st, mt, sq,
 ):
-    far, near = at_ref[0], at_ref[1].astype(f32)
+    place, place_f, near = at_ref[1], at_ref[1].astype(f32), at_ref[2].astype(f32)
     for m in range(0, ORDER, 2):
         rates = [row(dt, i) for i in (m, m + 1)]
         steps = [jnp.exp(-float(8 * ROWS) * d) for d in rates]
-        before, _ = scan_blocks(got_ref, m, steps, far)
+        far, _ = scan_blocks(got_ref, m, steps, 4, place)
+        halves = load_pair(half_ref, 0, m)
         for i in range(2):
-            entry = row(before_ref, m + i) + jnp.exp(-float(ROWS) * near * rates[i]) * before[i]
+            far_i = far[i] + jnp.exp(-float(8 * ROWS) * place_f * rates[i]) * halves[i]
+            entry = row(before_ref, m + i) + jnp.exp(-float(ROWS) * near * rates[i]) * far_i
             put(st, m + i, row(wt, m + i) * entry)
     pole = [jnp.exp(-d) for d in rows_of(dt, ORDER)]
     skip = skip_ref[...]
@@ -264,16 +274,17 @@
     modes = (ORDER * GROUPS, LANES)
     taps = (24 * GROUPS, LANES)
     blocks = (8 * ORDER * GROUPS, LANES)
+    quads = (4 * ORDER * GROUPS, LANES)
     whole = (ROWS * GROUPS, LANES)
     natural = (ROWS, query.shape[1])
     vmem = pltpu.VMEM
 
-    at = jnp.stack([lax.axis_index("z"), lax.axis_index("y")]).astype(jnp.int32)
+    at = jnp.stack([lax.axis_index(name) for name in CONTEXT]).astype(jnp.int32)
     tails, q_here, k_here, v_here = call(
         fetch, "fetch", [((24, natural[1]), bf16)] + [(natural, bf16)] * 3, [pltpu.SemaphoreType.DMA((2, 3))],
         3, far=(0, 1, 2), limit=LIMIT,
     )(query, key, value)
-    halo = lax.ppermute(tails, ("z", "y"), [(i, i + 1) for i in range(63)])
+    halo = lax.ppermute(tails, CONTEXT, [(i, i + 1) for i in range(63)])
     qc, own, clean, taps_t, heads, rates, weights, skip, gain = call(
         local_part, "local_part",
         [(whole, f32)] * 2 + [(modes, f32)] + [(taps, f32)] * 2 + [(modes, f32)] * 2
@@ -285,15 +296,24 @@
     )(halo, heads, taps_t, rates, clean)
     near = lax.all_to_all(sent, "y", 0, 0, tiled=True)
     totals, before = call(
-        scan_near, "scan_near", [(blocks, bf16), (modes, f32)], [], 3, 1,
+        scan_near, "scan_near", [(quads, bf16), (modes, f32)], [], 3, 1,
     )(at, near, rates)
-    far = lax.all_to_all(totals, "z", 0, 0, tiled=True)
+
+    def exchange(x, _):
+        return lax.all_to_all(x, "place", 0, 0, tiled=True)
+
+    totals, second = lax.optimization_barrier((totals, at[0]))
+    quad = lax.switch(second, (exchange, lambda x, _: x), totals, totals)
+    half, = call(sum_half, "sum_half", [(modes, bf16)], [], 2)(quad, rates)
+    carried = lax.ppermute(half, "half", [(0, 1)])
+    totals, half = lax.optimization_barrier((totals, half))
+    quad = lax.switch(second, (lambda _, y: y, exchange), totals, quad)
     mixed, scaled, squares = call(
         finish, "finish",
         [(natural, bf16), (natural, f32), ((8, LANES), f32)],
         [vmem(modes, f32), vmem((16 * GROUPS, LANES), f32), vmem((ROWS, LANES), f32)],
-        11, 1,
-    )(at, far, before, rates, weights, skip, qc, own, edge, residual, gain)
+        12, 1,
+    )(at, quad, carried, before, rates, weights, skip, qc, own, edge, residual, gain)
     gathered = lax.all_to_all(squares, "tensor", 0, 0, tiled=True)
     return call(
         normalise, "normalise", [(natural, bf16)] * 2, [vmem(natural, bf16), pltpu.SemaphoreType.DMA((3,))],
@@ -302,9 +322,8 @@
 
 
 def solution(mesh):
-    context = ("z", "y")
-    split = Mesh(mesh.devices.reshape(8, 8, 8), ("z", "y", "tensor"))
-    rows = P(context, "tensor")
+    split = Mesh(mesh.devices.reshape(2, 4, 8, 8), CONTEXT + ("tensor",))
+    rows = P(CONTEXT, "tensor")
     in_specs = (
         rows, rows, rows, P(None, None, "tensor"), P(None, "tensor"), P(None, "tensor"),
         P("tensor"), rows, P("tensor"),

time: 61.4 us -> 56.9 us (0.927)
  blocking collectives: 48.1 us -> 41.2 us
  starting transfers between devices: 4.03 us -> 5.46 us
  waiting for transfers between devices: 0.01 us -> 0.99 us
    all_to_all x1, blocking collectives: 19.4 us -> 11.5 us  [exchange(): return lax.all_to_all(x, 'place', 0, 0, tiled=True)]
    ppermute x1 -> x2, starting transfers between devices: 4.03 us -> 5.46 us  [the longest x1 4.03 us: shards(): halo = lax.ppermute(tails, CONTEXT, [(i, i + 1) for i in range(63)])]
    ppermute x1 -> x2, waiting for transfers between devices: 0.01 us -> 0.99 us  [the longest x1 0.99 us: shards(): carried = lax.ppermute(half, 'half', [(0, 1)])]
    all_to_all x1, blocking collectives: 13.6 us -> 14.5 us  [shards(): gathered = lax.all_to_all(squares, 'tensor', 0, 0, tiled=True)]
  transfers between devices with their start and end apart: 1 -> 2, of which waited for: 0 -> 1; matrix products, arithmetic and copies ran while one was open for 0% -> 0% of each run, Pallas kernels for 5% -> 5%
where the time goes in v2:
time: 56.9 us; the launch traced here: 56.6 us
  blocking collectives  41.2 us (72%)
  Pallas kernels  7.4 us (13%)
  starting transfers between devices  5.46 us (10%)
  waiting for transfers between devices  0.99 us (2%)
  between operations  0.74 us (1%)
  local copies, waits for them, and re-layouts  0.7 us (1%)
    all_to_all x1, blocking collectives, shards(): near = lax.all_to_all(sent, 'y', 0, 0, tiled=True)  15.1 us
    all_to_all x1, blocking collectives, shards(): gathered = lax.all_to_all(squares, 'tensor', 0, 0, tiled=True)  14.5 us
    all_to_all x1, blocking collectives, exchange(): return lax.all_to_all(x, 'place', 0, 0, tiled=True)  11.5 us
    ppermute x1, starting transfers between devices, shards(): halo = lax.ppermute(tails, CONTEXT, [(i, i + 1) for i in range(63)])  4.03 us
    pallas_call x1, Pallas kernels, shards(): call(local_part, 'local_part', [(whole, f32)] * 2 + [(modes, f32)] + [(ta...  2.77 us
    pallas_call x1, Pallas kernels, shards(): call(finish, 'finish', [(natural, bf16), (natural, f32), ((8, LANES), f32...  1.61 us
    ppermute x1, starting transfers between devices, shards(): carried = lax.ppermute(half, 'half', [(0, 1)])  1.42 us
    pallas_call x1, Pallas kernels, shards(): call(fetch, 'fetch', [((24, natural[1]), bf16)] + [(natural, bf16)] * 3,...  1.26 us
  transfers between devices with their start and end apart: 2, of which 1 were waited for; matrix products, arithmetic and copies ran while one was open for 0% of the time, Pallas kernels for 5%

profile of v2, /device:TPU:1, one launch (start us, length us, event | category | flops | bytes accessed | tf_op | source)
XLA Modules:
  0.0 56.6 jit_solution(15362726887791816851)
XLA Ops:
  0.6 0.0 copy-start.1
  0.6 0.0 copy-start.2
  0.7 0.0 copy-start.3
  0.7 1.3 %fetch.1 = (bf16[24,1024]{1,0:T(8,128)(2,1)S(1)}, bf16[128,1024]{1,0:T(8,128)(2,1)S(1)}, bf16[128,1024]{1,0:T(8,128)(2,1)S(1)}, bf16[128,1024]{1,0:T(8,128)(2,1)S(1)}) custom-call(bf16[128,1024]{1,0:T(8,128)(2,1)} %q_hbm.1, bf16[128,1024]{1,0:T(8,128)(2,1)} %k_hbm.1, bf16[128,1024]{1,0:T(8,128)(2,1)} %v_hbm.1), custom_call_target="tpu_custom_call" | custom-call | tf_op jit(solution)/shard_map/fetch/pallas_call | solution.py:283
  1.9 4.0 %collective-permute-start = (bf16[24,1024]{1,0:T(8,128)(2,1)S(1)}, bf16[24,1024]{1,0:T(8,128)(2,1)S(1)}, u32[]{:S(2)}, u32[]{:S(2)}) collective-permute-start(bf16[24,1024]{1,0:T(8,128)(2,1)S(1)} %get-tuple-element.35), channel_id=1, source_target_pairs={{0,8},{8,16},{16,24},{24,32},{32,40},{40,48},{48,56},{56,64},{64,7... | collective-permute-start | bytes 147464 | tf_op jit(solution)/shard_map/ppermute | solution.py:287
  6.0 0.1 pad_add_fusion.at_ref
  6.1 0.0 copy-done.1
  6.1 0.0 copy-done.2
  6.1 0.0 copy-done.3
  6.1 0.7 %copy-done.5 = f32[1024]{0:T(1024)S(1)} copy-done((f32[1024]{0:T(1024)S(1)}, f32[1024]{0:T(1024)}, u32[]{:S(2)}) %copy-start.5) | copy-done | bytes 4120
  6.7 0.0 copy-done.4
  6.8 2.8 %local_part.1 = (f32[1024,128]{1,0:T(8,128)S(1)}, f32[1024,128]{1,0:T(8,128)S(1)}, f32[128,128]{1,0:T(8,128)S(1)}, f32[192,128]{1,0:T(8,128)S(1)}, f32[192,128]{...) custom-call(s32[3]{0:T(128)S(1)} %pad_add_fusion.at_ref, ...), custom_call_target="tpu_custom_call" | custom-call | tf_op jit(solution)/shard_map/local_part/pallas_call | solution.py:288
  9.5 0.0 collective-permute-done.halo_ref
  9.5 0.1 edge_part.1
  9.6 15.1 %all_to_all.42 = bf16[8,128,128]{2,1,0:T(8,128)(2,1)S(1)} all-to-all(bf16[8,128,128]{2,1,0:T(8,128)(2,1)S(1)} %bitcast.16), channel_id=1, replica_groups=mesh['half'=2,'place'=4,'y'=8,'tensor'=8] {'y'}, dimensions={0} | all-to-all | bytes 524288 | tf_op jit(solution)/shard_map/all_to_all | solution.py:297
  24.8 0.6 %scan_near.1 = (bf16[512,128]{1,0:T(8,128)(2,1)S(1)}, f32[128,128]{1,0:T(8,128)S(1)}) custom-call(s32[3]{0:T(128)S(1)} %pad_add_fusion.at_ref, bf16[1024,128]{1,0:T(8,128)(2,1)S(1)} %bitcast.15, f32[128,128]{1,0:T(8,128)S(1)} %get-tuple-element.41.dt), custom_call_target="tpu_custom_call" | custom-call | tf_op jit(solution)/shard_map/scan_near/pallas_call | solution.py:298
  25.4 11.6 %conditional.2 = (bf16[512,128]{1,0:T(8,128)(2,1)S(1)}) conditional(s32[]{:T(128)} %clamp.4, bf16[512,128]{1,0:T(8,128)(2,1)S(1)} %get-tuple-element.47, bf16[512,128]{1,0:T(8,128)(2,1)S(1)} %get-tuple-element.47), branch_computations={%region_0.0_spmd, %region_1.0_spmd} | conditional | bytes 262152 | solution.py:306
  25.4 11.5 %all_to_all.40 = bf16[4,128,128]{2,1,0:T(8,128)(2,1)S(1)} all-to-all(bf16[4,128,128]{2,1,0:T(8,128)(2,1)S(1)} %bitcast.23), channel_id=1, replica_groups=mesh['half'=2,'place'=4,'y'=8,'tensor'=8] {'place'}, dimensions={0} | all-to-all | bytes 262144 | tf_op jit(solution)/shard_map/cond/branch_0_fun/all_to_all | solution.py:303
  37.0 1.4 %collective-permute-start.1 = (bf16[128,128]{1,0:T(8,128)(2,1)S(1)}, bf16[128,128]{1,0:T(8,128)(2,1)S(1)}, u32[]{:S(2)}, u32[]{:S(2)}) collective-permute-start(bf16[128,128]{1,0:T(8,128)(2,1)S(1)} %sum_half.1), channel_id=1, source_target_pairs={{0,256},{1,257},{2,258},{3,259},{4,260},{5,261},{6,262},{7,263},{8... | collective-permute-start | bytes 98312 | tf_op jit(solution)/shard_map/ppermute | solution.py:308
  38.4 1.0 %collective-permute-done.1.half_ref = bf16[128,128]{1,0:T(8,128)(2,1)S(1)} collective-permute-done((bf16[128,128]{1,0:T(8,128)(2,1)S(1)}, bf16[128,128]{1,0:T(8,128)(2,1)S(1)}, u32[]{:S(2)}, u32[]{:S(2)}) %collective-permute-start.1) | collective-permute-done | bytes 32800 | tf_op jit(solution)/shard_map/ppermute | solution.py:308
  39.4 0.0 copy-done
  39.4 1.6 %finish.1 = (bf16[128,1024]{1,0:T(8,128)(2,1)S(1)}, f32[128,1024]{1,0:T(8,128)S(1)}, f32[8,128]{1,0:T(8,128)S(1)}) custom-call(s32[3]{0:T(128)S(1)} %pad_add_fusion.at_ref, bf16[512,128]{1,0:T(8,128)(2,1)S(1)} %get-tuple-element.59.got_ref, bf16[128,128]{1,0:T(8,128)(2,1)S(1)} %collective-permute-done.1.half_ref, ...), custom_call_target="tpu_custom_call" | custom-call | tf_op jit(solution)/shard_map/finish/pallas_call | solution.py:311
  41.0 14.5 %all_to_all.43 = f32[8,1,128]{2,1,0:T(1,128)S(1)} all-to-all(f32[8,1,128]{2,1,0:T(1,128)S(1)} %bitcast.20), channel_id=1, replica_groups=mesh['half'=2,'place'=4,'y'=8,'tensor'=8] {'tensor'}, dimensions={0} | all-to-all | bytes 8192 | tf_op jit(solution)/shard_map/all_to_all | solution.py:317
  55.6 1.0 %normalise.1 = (bf16[128,1024]{1,0:T(8,128)(2,1)}, bf16[128,1024]{1,0:T(8,128)(2,1)}) custom-call(bf16[128,1024]{1,0:T(8,128)(2,1)S(1)} %get-tuple-element.55.mixed_ref, f32[128,1024]{1,0:T(8,128)S(1)} %get-tuple-element.56.scaled_ref, f32[8,128]{1,0:T(8,128)S(1)} %bitcast.17), custom_call_target="tpu_custom_call" | custom-call | tf_op jit(solution)/shard_map/normalise/pallas_call | solution.py:318
  (5 shorter events, 0.1 us)
Async XLA Ops:
  0.6 5.4 %copy-start.1 = (f32[3,7,1024]{2,1,0:T(8,128)S(1)}, f32[3,7,1024]{2,1,0:T(8,128)}, u32[]{:S(2)}) copy-start(f32[3,7,1024]{2,1,0:T(8,128)} %f_ref.1) | copy-start | bytes 258052
  0.6 5.4 %copy-start.2 = (f32[16,1024]{1,0:T(8,128)S(1)}, f32[16,1024]{1,0:T(8,128)}, u32[]{:S(2)}) copy-start(f32[16,1024]{1,0:T(8,128)} %d_ref.1) | copy-start | bytes 196612
  0.7 5.4 %copy-start.3 = (f32[16,1024]{1,0:T(8,128)S(1)}, f32[16,1024]{1,0:T(8,128)}, u32[]{:S(2)}) copy-start(f32[16,1024]{1,0:T(8,128)} %r_ref.1) | copy-start | bytes 196612
  1.9 7.6 %collective-permute-start = (bf16[24,1024]{1,0:T(8,128)(2,1)S(1)}, bf16[24,1024]{1,0:T(8,128)(2,1)S(1)}, u32[]{:S(2)}, u32[]{:S(2)}) collective-permute-start(bf16[24,1024]{1,0:T(8,128)(2,1)S(1)} %get-tuple-element.35), channel_id=1, source_target_pairs={{0,8},{8,16},{16,24},{24,32},{32,40},{40,48},{48,56},{56,64},{64,7... | collective-permute-start | bytes 147464 | tf_op jit(solution)/shard_map/ppermute | solution.py:287
  6.0 0.7 %copy-start.5 = (f32[1024]{0:T(1024)S(1)}, f32[1024]{0:T(1024)}, u32[]{:S(2)}) copy-start(f32[1024]{0:T(1024)} %param.21) | copy-start | bytes 12292
  6.0 0.7 %copy-start.4 = (f32[1024]{0:T(1024)S(1)}, f32[1024]{0:T(1024)}, u32[]{:S(2)}) copy-start(f32[1024]{0:T(1024)} %param.19) | copy-start | bytes 12292
  36.9 2.5 %copy-start = (bf16[128,1024]{1,0:T(8,128)(2,1)S(1)}, bf16[128,1024]{1,0:T(8,128)(2,1)}, u32[]{:S(2)}) copy-start(bf16[128,1024]{1,0:T(8,128)(2,1)} %residual_ref.1) | copy-start | bytes 786436
  37.0 2.4 %collective-permute-start.1 = (bf16[128,128]{1,0:T(8,128)(2,1)S(1)}, bf16[128,128]{1,0:T(8,128)(2,1)S(1)}, u32[]{:S(2)}, u32[]{:S(2)}) collective-permute-start(bf16[128,128]{1,0:T(8,128)(2,1)S(1)} %sum_half.1), channel_id=1, source_target_pairs={{0,256},{1,257},{2,258},{3,259},{4,260},{5,261},{6,262},{7,263},{8... | collective-permute-start | bytes 98312 | tf_op jit(solution)/shard_map/ppermute | solution.py:308

commit v3 on v2

--- a/solution.py
+++ b/solution.py
@@ -13,6 +13,7 @@
 GROUPS = 8
 LIMIT = 54300 << 10
 CONTEXT = ("half", "place", "y")
+Z = CONTEXT[:2]
 BLOCK = 8
 
 f32 = jnp.float32
@@ -177,29 +178,31 @@
     return before, total
 
 
-def scan_near(at_ref, got_ref, dt, out_ref, before_ref):
+def scan_near(at_ref, got_ref, dt, out_ref, total_ref, step_ref, before_ref):
     index = at_ref[2]
     for m in range(0, ORDER, 2):
         steps = [jnp.exp(-float(ROWS) * row(dt, i)) for i in (m, m + 1)]
         before, total = scan_blocks(got_ref, m, steps, 8, index)
         for i in range(2):
             put(before_ref, m + i, before[i])
+            put(step_ref, m + i, jnp.exp(-float(8 * ROWS) * row(dt, m + i)))
         both = jnp.concatenate(total, axis=0).astype(bf16)
+        total_ref[m * GROUPS : (m + 2) * GROUPS, :] = both
         for copy in range(4):
             out_ref[(copy * ORDER + m) * GROUPS : (copy * ORDER + m + 2) * GROUPS, :] = both
 
 
-def sum_half(got_ref, dt, out_ref):
-    for m in range(0, ORDER, 2):
-        steps = [jnp.exp(-float(8 * ROWS) * row(dt, i)) for i in (m, m + 1)]
-        _, total = scan_blocks(got_ref, m, steps, 4)
-        out_ref[m * GROUPS : (m + 2) * GROUPS, :] = jnp.concatenate(total, axis=0).astype(bf16)
-
-
-def finish(
-    at_ref, got_ref, half_ref, before_ref, dt, wt, skip_ref, qc_ref, g_ref, edge_ref, residual_ref, gain_ref,
-    mixed_ref, scaled_ref, squares_ref, st, mt, sq,
-):
+def finish_lower(at_ref, far_ref, before_ref, dt, wt, *refs):
+    st = refs[-3]
+    near = at_ref[2].astype(f32)
+    for m in range(ORDER):
+        entry = row(before_ref, m) + jnp.exp(-float(ROWS) * near * row(dt, m)) * row(far_ref, m)
+        put(st, m, row(wt, m) * entry)
+    gate(dt, wt, *refs)
+
+
+def finish_upper(at_ref, got_ref, half_ref, before_ref, dt, wt, *refs):
+    st = refs[-3]
     place, place_f, near = at_ref[1], at_ref[1].astype(f32), at_ref[2].astype(f32)
     for m in range(0, ORDER, 2):
         rates = [row(dt, i) for i in (m, m + 1)]
@@ -210,6 +213,13 @@
             far_i = far[i] + jnp.exp(-float(8 * ROWS) * place_f * rates[i]) * halves[i]
             entry = row(before_ref, m + i) + jnp.exp(-float(ROWS) * near * rates[i]) * far_i
             put(st, m + i, row(wt, m + i) * entry)
+    gate(dt, wt, *refs)
+
+
+def gate(
+    dt, wt, skip_ref, qc_ref, g_ref, edge_ref, residual_ref, gain_ref,
+    mixed_ref, scaled_ref, squares_ref, st, mt, sq,
+):
     pole = [jnp.exp(-d) for d in rows_of(dt, ORDER)]
     skip = skip_ref[...]
     count = 16
@@ -295,26 +305,52 @@
         edge_part, "edge_part", [(blocks, bf16), ((16 * GROUPS, LANES), f32)], [vmem((48 * GROUPS, LANES), f32)], 5,
     )(halo, heads, taps_t, rates, clean)
     near = lax.all_to_all(sent, "y", 0, 0, tiled=True)
-    totals, before = call(
-        scan_near, "scan_near", [(quads, bf16), (modes, f32)], [], 3, 1,
+    quads_out, total, step, before = call(
+        scan_near, "scan_near", [(quads, bf16), (modes, bf16), (modes, f32), (modes, f32)], [], 3, 1,
     )(at, near, rates)
-
-    def exchange(x, _):
-        return lax.all_to_all(x, "place", 0, 0, tiled=True)
-
-    totals, second = lax.optimization_barrier((totals, at[0]))
-    quad = lax.switch(second, (exchange, lambda x, _: x), totals, totals)
-    half, = call(sum_half, "sum_half", [(modes, bf16)], [], 2)(quad, rates)
-    carried = lax.ppermute(half, "half", [(0, 1)])
-    totals, half = lax.optimization_barrier((totals, half))
-    quad = lax.switch(second, (lambda _, y: y, exchange), totals, quad)
-    mixed, scaled, squares = call(
-        finish, "finish",
-        [(natural, bf16), (natural, f32), ((8, LANES), f32)],
-        [vmem(modes, f32), vmem((16 * GROUPS, LANES), f32), vmem((ROWS, LANES), f32)],
-        12, 1,
-    )(at, quad, carried, before, rates, weights, skip, qc, own, edge, residual, gain)
-    gathered = lax.all_to_all(squares, "tensor", 0, 0, tiled=True)
+    total, upper_half, place = lax.optimization_barrier((total, at[0], at[1]))
+    z = 4 * upper_half + place
+    even = lax.rem(z, 2) == 0
+
+    def swapped(first):
+        return lambda t, _: lax.ppermute(t, Z, [(first, first + 1), (first + 1, first)])
+
+    def summed(mine, other):
+        mine, other = mine.astype(f32), other.astype(f32)
+        return step * jnp.where(even, mine, other) + jnp.where(even, other, mine)
+
+    other = lax.cond(z < 2, swapped(0), lambda _, o: o, total, total)
+    pair = summed(total, other).astype(bf16)
+    arrived = lax.ppermute(pair, Z, [(0, 2), (1, 3)])
+    total, pair = lax.optimization_barrier((total, pair))
+    other = lax.cond((z == 2) | (z == 3), swapped(2), lambda _, o: o, total, other)
+    arrived = arrived.astype(f32)
+    four = (step * step * arrived + summed(total, other)).astype(bf16)
+    carried = lax.ppermute(four, Z, [(2, 6), (3, 7)]), lax.ppermute(four, Z, [(2, 4), (3, 5)])
+    far = jnp.where(even, arrived, step * arrived + other.astype(f32))
+    quads_out, far, four = lax.optimization_barrier((quads_out, far, four))
+
+    def finished(body, count, *own_args):
+        mixed, scaled, squares = call(
+            body, body.__name__,
+            [(natural, bf16), (natural, f32), ((8, LANES), f32)],
+            [vmem(modes, f32), vmem((16 * GROUPS, LANES), f32), vmem((ROWS, LANES), f32)],
+            count, 1,
+        )(at, *own_args, before, rates, weights, skip, qc, own, edge, residual, gain)
+        return mixed, scaled, lax.all_to_all(squares, "tensor", 0, 0, tiled=True)
+
+    def lower(_):
+        return finished(finish_lower, 11, far), quads_out
+
+    def upper(_):
+        nothing = jnp.zeros(natural, bf16), jnp.zeros(natural, f32), jnp.zeros((8, LANES), f32)
+        return nothing, lax.all_to_all(quads_out, "place", 0, 0, tiled=True)
+
+    done, quad = lax.cond(z < 4, lower, upper, 0)
+    carried = carried[0] + carried[1]
+    mixed, scaled, gathered = lax.cond(
+        z < 4, lambda d: d, lambda d: finished(finish_upper, 12, quad, carried), done
+    )
     return call(
         normalise, "normalise", [(natural, bf16)] * 2, [vmem(natural, bf16), pltpu.SemaphoreType.DMA((3,))],
         3, far_out=True,

time: 56.9 us -> 55.9 us (0.982)
  the two profiles are of different devices: /device:TPU:1 before, /device:TPU:256 now
where the time goes in v3:
time: 55.9 us; the launch traced here: 55.4 us
  blocking collectives  35.2 us (63%)
  Pallas kernels  7.36 us (13%)
  starting transfers between devices  6.1 us (11%)
  waiting for transfers between devices  2.26 us (4%)
  local copies, waits for them, and re-layouts  1.96 us (4%)
  other arithmetic  1.66 us (3%)
  between operations  0.8 us (1%)
    all_to_all x1, blocking collectives, shards(): near = lax.all_to_all(sent, 'y', 0, 0, tiled=True)  15.5 us
    all_to_all x1, blocking collectives, upper(): return (nothing, lax.all_to_all(quads_out, 'place', 0, 0, tiled=True))  10.3 us
    all_to_all x1, blocking collectives, finished(): return (mixed, scaled, lax.all_to_all(squares, 'tensor', 0, 0, tiled=True))  9.38 us
    ppermute x1, starting transfers between devices, shards(): halo = lax.ppermute(tails, CONTEXT, [(i, i + 1) for i in range(63)])  3.48 us
    pallas_call x1, Pallas kernels, shards(): call(local_part, 'local_part', [(whole, f32)] * 2 + [(modes, f32)] + [(ta...  2.77 us
    ppermute x1, waiting for transfers between devices, shards(): halo = lax.ppermute(tails, CONTEXT, [(i, i + 1) for i in range(63)])  2.25 us
    pallas_call x1, Pallas kernels, finished(): call(body, body.__name__, [(natural, bf16), (natural, f32), ((8, LANES),...  1.61 us
    ppermute x1, starting transfers between devices, shards(): lax.ppermute(four, Z, [(2, 4), (3, 5)])  1.29 us
  transfers between devices with their start and end apart: 4, of which 1 were waited for; matrix products, arithmetic and copies ran while one was open for 1% of the time, Pallas kernels for 5%

profile of v3, /device:TPU:256, one launch (start us, length us, event | category | flops | bytes accessed | tf_op | source)
XLA Modules:
  0.0 55.4 jit_solution(5945773186108676264)
XLA Ops:
  0.7 1.3 %fetch.1 = (bf16[24,1024]{1,0:T(8,128)(2,1)S(1)}, bf16[128,1024]{1,0:T(8,128)(2,1)S(1)}, bf16[128,1024]{1,0:T(8,128)(2,1)S(1)}, bf16[128,1024]{1,0:T(8,128)(2,1)S(1)}) custom-call(bf16[128,1024]{1,0:T(8,128)(2,1)} %q_hbm.1, bf16[128,1024]{1,0:T(8,128)(2,1)} %k_hbm.1, bf16[128,1024]{1,0:T(8,128)(2,1)} %v_hbm.1), custom_call_target="tpu_custom_call" | custom-call | tf_op jit(solution)/shard_map/fetch/pallas_call | solution.py:293
  1.9 3.5 %collective-permute-start.2 = (bf16[24,1024]{1,0:T(8,128)(2,1)S(1)}, bf16[24,1024]{1,0:T(8,128)(2,1)S(1)}, u32[]{:S(2)}, u32[]{:S(2)}) collective-permute-start(bf16[24,1024]{1,0:T(8,128)(2,1)S(1)} %get-tuple-element.139), channel_id=1, source_target_pairs={{0,8},{8,16},{16,24},{24,32},{32,40},{40,48},{48,56},{56,64},{64,7... | collective-permute-start | bytes 147464 | tf_op jit(solution)/shard_map/ppermute | solution.py:297
  5.4 0.1 pad_add_fusion.at_ref
  5.5 0.7 %copy-done.4 = f32[1024]{0:T(1024)S(1)} copy-done((f32[1024]{0:T(1024)S(1)}, f32[1024]{0:T(1024)}, u32[]{:S(2)}) %copy-start.4) | copy-done | bytes 4120
  6.2 0.0 copy-done.3
  6.2 2.8 %local_part.1 = (f32[1024,128]{1,0:T(8,128)S(1)}, f32[1024,128]{1,0:T(8,128)S(1)}, f32[128,128]{1,0:T(8,128)S(1)}, f32[192,128]{1,0:T(8,128)S(1)}, f32[192,128]{...) custom-call(s32[3]{0:T(128)S(1)} %pad_add_fusion.at_ref, ...), custom_call_target="tpu_custom_call" | custom-call | tf_op jit(solution)/shard_map/local_part/pallas_call | solution.py:298
  9.0 2.2 %collective-permute-done.2.halo_ref = bf16[24,1024]{1,0:T(8,128)(2,1)S(1)} collective-permute-done((bf16[24,1024]{1,0:T(8,128)(2,1)S(1)}, bf16[24,1024]{1,0:T(8,128)(2,1)S(1)}, u32[]{:S(2)}, u32[]{:S(2)}) %collective-permute-start.2) | collective-permute-done | bytes 49184 | tf_op jit(solution)/shard_map/ppermute | solution.py:297
  11.2 0.1 edge_part.1
  11.3 15.5 %all_to_all.40 = bf16[8,128,128]{2,1,0:T(8,128)(2,1)S(1)} all-to-all(bf16[8,128,128]{2,1,0:T(8,128)(2,1)S(1)} %bitcast.18), channel_id=1, replica_groups=mesh['half'=2,'place'=4,'y'=8,'tensor'=8] {'y'}, dimensions={0} | all-to-all | bytes 524288 | tf_op jit(solution)/shard_map/all_to_all | solution.py:307
  26.8 0.6 %scan_near.1 = (bf16[512,128]{1,0:T(8,128)(2,1)S(1)}, bf16[128,128]{1,0:T(8,128)(2,1)S(1)}, f32[128,128]{1,0:T(8,128)S(1)}, f32[128,128]{1,0:T(8,128)S(1)}) custom-call(s32[3]{0:T(128)S(1)} %pad_add_fusion.at_ref, bf16[1024,128]{1,0:T(8,128)(2,1)S(1)} %bitcast.17, f32[128,128]{1,0:T(8,128)S(1)} %get-tuple-element.145.dt), custom_call_target="tpu_custom_call" | custom-call | tf_op jit(solution)/shard_map/scan_near/pallas_call | solution.py:308
  27.5 0.6 %conditional.4 = (bf16[128,128]{1,0:T(8,128)(2,1)}) conditional(s32[]{:T(128)} %convert_element_type.40, bf16[128,128]{1,0:T(8,128)(2,1)S(1)} %get-tuple-element.153, bf16[128,128]{1,0:T(8,128)(2,1)S(1)} %get-tuple-element.153), branch_computations={%region_0.0_spmd, %region_1.0_spmd} | conditional | bytes 131120 | solution.py:322
  27.5 0.6 %copy.13 = bf16[128,128]{1,0:T(8,128)(2,1)} copy(bf16[128,128]{1,0:T(8,128)(2,1)S(1)} %param) | data formatting | bytes 65536 | tf_op jit(solution)/shard_map/cond
  28.1 0.8 %fusion.2 = bf16[128,128]{1,0:T(8,128)(2,1)S(1)} fusion(f32[128,128]{1,0:T(8,128)S(1)} %get-tuple-element.151, bf16[128,128]{1,0:T(8,128)(2,1)} %get-tuple-element.187, bf16[128,128]{1,0:T(8,128)(2,1)S(1)} %get-tuple-element.153, pred[]{:T(512)S(6)} %eq.9), kind=kLoop, calls=%fused_computation.10 | loop fusion | flops 114688 | bytes 163841 | tf_op jit(solution)/shard_map/convert_element_type | solution.py:323
  28.9 0.7 %collective-permute-start.3 = (bf16[128,128]{1,0:T(8,128)(2,1)S(1)}, bf16[128,128]{1,0:T(8,128)(2,1)S(1)}, u32[]{:S(2)}, u32[]{:S(2)}) collective-permute-start(bf16[128,128]{1,0:T(8,128)(2,1)S(1)} %fusion.2), channel_id=1, source_target_pairs={{0,128},{64,192},{1,129},{65,193},{2,130},{66,194},{3,131},{67,195... | collective-permute-start | bytes 98312 | tf_op jit(solution)/shard_map/ppermute | solution.py:324
  29.6 0.8 %convert_select_fusion.2 = (f32[128,128]{1,0:T(8,128)S(1)}, bf16[128,128]{1,0:T(8,128)(2,1)S(1)}) fusion(bf16[128,128]{1,0:T(8,128)(2,1)S(1)} %collective-permute-done.3, bf16[128,128]{1,0:T(8,128)(2,1)} %get-tuple-element.188, f32[128,128]{1,0:T(8,128)S(1)} %get-tuple-element.151, pred[]{:T(512)S(6)} %eq.9, bf16[128,128]{1,0:T(8,128)(2,1)S(1)} %get-tuple-element.153), kind=kLoop, calls=%fused_computation.3 | loop fusion | flops 229376 | bytes 262145 | tf_op jit(solution)/shard_map/jit(_where)/select_n | solution.py:330
  30.4 0.7 %collective-permute-start.4 = (bf16[128,128]{1,0:T(8,128)(2,1)S(1)}, bf16[128,128]{1,0:T(8,128)(2,1)S(1)}, u32[]{:S(2)}, u32[]{:S(2)}) collective-permute-start(bf16[128,128]{1,0:T(8,128)(2,1)S(1)} %get-tuple-element.172), channel_id=1, source_target_pairs={{128,384},{192,448},{129,385},{193,449},{130,386},{194,450},{131,3... | collective-permute-start | bytes 98312 | tf_op jit(solution)/shard_map/ppermute | solution.py:329
  31.1 1.3 %collective-permute-start.5 = (bf16[128,128]{1,0:T(8,128)(2,1)S(1)}, bf16[128,128]{1,0:T(8,128)(2,1)S(1)}, u32[]{:S(2)}, u32[]{:S(2)}) collective-permute-start(bf16[128,128]{1,0:T(8,128)(2,1)S(1)} %get-tuple-element.172), channel_id=1, source_target_pairs={{128,256},{192,320},{129,257},{193,321},{130,258},{194,322},{131,2... | collective-permute-start | bytes 98312 | tf_op jit(solution)/shard_map/ppermute | solution.py:329
  32.4 11.0 %conditional.6 = (bf16[128,1024]{1,0:T(8,128)(2,1)S(1)}, f32[128,1024]{1,0:T(8,128)S(1)}, f32[8,128]{1,0:T(8,128)}, bf16[512,128]{1,0:T(8,128)(2,1)S(1)}) conditional(s32[]{:T(128)} %convert_element_type.38, bf16[512,128]{1,0:T(8,128)(2,1)S(1)} %get-tuple-element.155, (s32[3]{0:T(128)S(1)}, f32[128,128]{1,0:T(8,128)S(1)}, f32[128,128]{1,0:T(8,128)S(1)}, ...), branch_computations={%region_4.5_spmd, %region_5.6_spmd} | conditional | bytes 1314858 | solution.py:349
  32.4 10.3 %all_to_all.38 = bf16[4,128,128]{2,1,0:T(8,128)(2,1)S(1)} all-to-all(bf16[4,128,128]{2,1,0:T(8,128)(2,1)S(1)} %copy.31), channel_id=1, replica_groups=mesh['half'=2,'place'=4,'y'=8,'tensor'=8] {'place'}, dimensions={0} | all-to-all | bytes 262144 | tf_op jit(solution)/shard_map/cond/branch_0_fun/all_to_all | solution.py:347
  42.8 0.6 %broadcast.9 = f32[8,128]{1,0:T(8,128)} broadcast(f32[]{:T(128)} %constant.9.clone), dimensions={} | broadcast | bytes 4100 | tf_op jit(solution)/shard_map/broadcast.3
  43.4 11.0 %conditional.7 = (bf16[128,1024]{1,0:T(8,128)(2,1)S(1)}, f32[128,1024]{1,0:T(8,128)S(1)}, f32[8,128]{1,0:T(8,128)S(1)}) conditional(s32[]{:T(128)} %convert_element_type.38, (bf16[128,128]{1,0:T(8,128)(2,1)S(1)}, bf16[128,128]{1,0:T(8,128)(2,1)S(1)}, s32[3]{0:T(128)S(1)}, bf16[512,128]{1,0:T(8,128)(2,1)S(1)}, f32[128,128]{1,0:T(8,128)S(1)}, ...), branch_computations={%region_6.7_spmd, %region_7.8_spmd} | conditional | flops 16384 | bytes 106520 | solution.py:351
  43.4 1.6 %finish_upper.1 = (bf16[128,1024]{1,0:T(8,128)(2,1)S(1)}, f32[128,1024]{1,0:T(8,128)S(1)}, f32[8,128]{1,0:T(8,128)S(1)}) custom-call(s32[3]{0:T(128)S(1)} %get-tuple-element.89.at_ref, bf16[512,128]{1,0:T(8,128)(2,1)S(1)} %get-tuple-element.90.got_ref, bf16[128,128]{1,0:T(8,128)(2,1)S(1)} %add.13.half_ref, f32[128,128]{1,0:T(8,128)S(1)} %get-tuple-element.93.before_ref, ...), custom_call_target="tpu_custom_call" | custom-call | tf_op jit(solution)/shard_map/cond/branch_0_fun/finish_upper/pallas_call | solution.py:334
  45.0 9.4 %all_to_all.39 = f32[8,1,128]{2,1,0:T(1,128)S(1)} all-to-all(f32[8,1,128]{2,1,0:T(1,128)S(1)} %bitcast.21), channel_id=1, replica_groups=mesh['half'=2,'place'=4,'y'=8,'tensor'=8] {'tensor'}, dimensions={0} | all-to-all | bytes 8192 | tf_op jit(solution)/shard_map/cond/branch_0_fun/all_to_all | solution.py:340
  54.4 1.0 %normalise.1 = (bf16[128,1024]{1,0:T(8,128)(2,1)}, bf16[128,1024]{1,0:T(8,128)(2,1)}) custom-call(bf16[128,1024]{1,0:T(8,128)(2,1)S(1)} %get-tuple-element.168.mixed_ref, f32[128,1024]{1,0:T(8,128)S(1)} %get-tuple-element.169.scaled_ref, f32[8,128]{1,0:T(8,128)S(1)} %get-tuple-element.170.squares_ref), custom_call_target="tpu_custom_call" | custom-call | tf_op jit(solution)/shard_map/normalise/pallas_call | solution.py:354
  (18 shorter events, 0.1 us)
Async XLA Ops:
  0.6 4.9 %copy-start = (f32[3,7,1024]{2,1,0:T(8,128)S(1)}, f32[3,7,1024]{2,1,0:T(8,128)}, u32[]{:S(2)}) copy-start(f32[3,7,1024]{2,1,0:T(8,128)} %f_ref.1) | copy-start | bytes 258052
  0.6 4.9 %copy-start.1 = (f32[16,1024]{1,0:T(8,128)S(1)}, f32[16,1024]{1,0:T(8,128)}, u32[]{:S(2)}) copy-start(f32[16,1024]{1,0:T(8,128)} %d_ref.1) | copy-start | bytes 196612
  0.7 4.9 %copy-start.2 = (f32[16,1024]{1,0:T(8,128)S(1)}, f32[16,1024]{1,0:T(8,128)}, u32[]{:S(2)}) copy-start(f32[16,1024]{1,0:T(8,128)} %r_ref.1) | copy-start | bytes 196612
  1.9 9.3 %collective-permute-start.2 = (bf16[24,1024]{1,0:T(8,128)(2,1)S(1)}, bf16[24,1024]{1,0:T(8,128)(2,1)S(1)}, u32[]{:S(2)}, u32[]{:S(2)}) collective-permute-start(bf16[24,1024]{1,0:T(8,128)(2,1)S(1)} %get-tuple-element.139), channel_id=1, source_target_pairs={{0,8},{8,16},{16,24},{24,32},{32,40},{40,48},{48,56},{56,64},{64,7... | collective-permute-start | bytes 147464 | tf_op jit(solution)/shard_map/ppermute | solution.py:297
  5.5 0.7 %copy-start.4 = (f32[1024]{0:T(1024)S(1)}, f32[1024]{0:T(1024)}, u32[]{:S(2)}) copy-start(f32[1024]{0:T(1024)} %param.25) | copy-start | bytes 12292
  5.5 0.7 %copy-start.3 = (f32[1024]{0:T(1024)S(1)}, f32[1024]{0:T(1024)}, u32[]{:S(2)}) copy-start(f32[1024]{0:T(1024)} %param.23) | copy-start | bytes 12292
  27.5 4.9 %copy-start.5 = (bf16[128,1024]{1,0:T(8,128)(2,1)S(1)}, bf16[128,1024]{1,0:T(8,128)(2,1)}, u32[]{:S(2)}) copy-start(bf16[128,1024]{1,0:T(8,128)(2,1)} %param.24) | copy-start | bytes 786436
  28.9 0.7 %collective-permute-start.3 = (bf16[128,128]{1,0:T(8,128)(2,1)S(1)}, bf16[128,128]{1,0:T(8,128)(2,1)S(1)}, u32[]{:S(2)}, u32[]{:S(2)}) collective-permute-start(bf16[128,128]{1,0:T(8,128)(2,1)S(1)} %fusion.2), channel_id=1, source_target_pairs={{0,128},{64,192},{1,129},{65,193},{2,130},{66,194},{3,131},{67,195... | collective-permute-start | bytes 98312 | tf_op jit(solution)/shard_map/ppermute | solution.py:324
  30.4 13.0 %collective-permute-start.4 = (bf16[128,128]{1,0:T(8,128)(2,1)S(1)}, bf16[128,128]{1,0:T(8,128)(2,1)S(1)}, u32[]{:S(2)}, u32[]{:S(2)}) collective-permute-start(bf16[128,128]{1,0:T(8,128)(2,1)S(1)} %get-tuple-element.172), channel_id=1, source_target_pairs={{128,384},{192,448},{129,385},{193,449},{130,386},{194,450},{131,3... | collective-permute-start | bytes 98312 | tf_op jit(solution)/shard_map/ppermute | solution.py:329
  31.1 12.3 %collective-permute-start.5 = (bf16[128,128]{1,0:T(8,128)(2,1)S(1)}, bf16[128,128]{1,0:T(8,128)(2,1)S(1)}, u32[]{:S(2)}, u32[]{:S(2)}) collective-permute-start(bf16[128,128]{1,0:T(8,128)(2,1)S(1)} %get-tuple-element.172), channel_id=1, source_target_pairs={{128,256},{192,320},{129,257},{193,321},{130,258},{194,322},{131,2... | collective-permute-start | bytes 98312 | tf_op jit(solution)/shard_map/ppermute | solution.py:329

commit v4 on v3

--- a/solution.py
+++ b/solution.py
@@ -319,37 +319,44 @@
         mine, other = mine.astype(f32), other.astype(f32)
         return step * jnp.where(even, mine, other) + jnp.where(even, other, mine)
 
-    other = lax.cond(z < 2, swapped(0), lambda _, o: o, total, total)
-    pair = summed(total, other).astype(bf16)
-    arrived = lax.ppermute(pair, Z, [(0, 2), (1, 3)])
-    total, pair = lax.optimization_barrier((total, pair))
-    other = lax.cond((z == 2) | (z == 3), swapped(2), lambda _, o: o, total, other)
-    arrived = arrived.astype(f32)
-    four = (step * step * arrived + summed(total, other)).astype(bf16)
+    def by_pairs(total):
+        other = lax.cond(z < 2, swapped(0), lambda _, o: o, total, total)
+        pair = summed(total, other).astype(bf16)
+        arrived = lax.ppermute(pair, Z, [(0, 2), (1, 3)])
+        total, pair = lax.optimization_barrier((total, pair))
+        other = lax.cond(z < 2, lambda _, o: o, swapped(2), total, other)
+        arrived = arrived.astype(f32)
+        four = (step * step * arrived + summed(total, other)).astype(bf16)
+        return four, jnp.where(even, arrived, step * arrived + other.astype(f32))
+
+    def unwritten(after, *outs):
+        return call(lambda *_: None, "unwritten", outs, [], 1)(after)
+
+    four, far = lax.cond(z < 4, by_pairs, lambda t: unwritten(t, (modes, bf16), (modes, f32)), total)
     carried = lax.ppermute(four, Z, [(2, 6), (3, 7)]), lax.ppermute(four, Z, [(2, 4), (3, 5)])
-    far = jnp.where(even, arrived, step * arrived + other.astype(f32))
     quads_out, far, four = lax.optimization_barrier((quads_out, far, four))
+    results = (natural, bf16), (natural, f32), ((8, LANES), f32)
 
     def finished(body, count, *own_args):
         mixed, scaled, squares = call(
-            body, body.__name__,
-            [(natural, bf16), (natural, f32), ((8, LANES), f32)],
+            body, body.__name__, results,
             [vmem(modes, f32), vmem((16 * GROUPS, LANES), f32), vmem((ROWS, LANES), f32)],
             count, 1,
         )(at, *own_args, before, rates, weights, skip, qc, own, edge, residual, gain)
         return mixed, scaled, lax.all_to_all(squares, "tensor", 0, 0, tiled=True)
 
     def lower(_):
-        return finished(finish_lower, 11, far), quads_out
+        done = finished(finish_lower, 11, far)
+        return *done, *unwritten(done[2], (quads, bf16))
 
     def upper(_):
-        nothing = jnp.zeros(natural, bf16), jnp.zeros(natural, f32), jnp.zeros((8, LANES), f32)
-        return nothing, lax.all_to_all(quads_out, "place", 0, 0, tiled=True)
-
-    done, quad = lax.cond(z < 4, lower, upper, 0)
+        quad = lax.all_to_all(quads_out, "place", 0, 0, tiled=True)
+        return *unwritten(quad, *results), quad
+
+    *done, quad = lax.cond(z < 4, lower, upper, 0)
     carried = carried[0] + carried[1]
     mixed, scaled, gathered = lax.cond(
-        z < 4, lambda d: d, lambda d: finished(finish_upper, 12, quad, carried), done
+        z < 4, lambda d: d, lambda _: finished(finish_upper, 12, quad, carried), tuple(done)
     )
     return call(
         normalise, "normalise", [(natural, bf16)] * 2, [vmem(natural, bf16), pltpu.SemaphoreType.DMA((3,))],

time: 55.9 us -> 54.1 us (0.968)
  the two profiles are of different devices: /device:TPU:256 before, /device:TPU:1 now
where the time goes in v4:
time: 54.1 us; the launch traced here: 53.3 us
  blocking collectives  28.9 us (53%)
  starting transfers between devices  10.8 us (20%)
  Pallas kernels  8.69 us (16%)
  waiting for transfers between devices  1.63 us (3%)
  local copies, waits for them, and re-layouts  1.46 us (3%)
  other arithmetic  0.89 us (2%)
  between operations  0.76 us (1%)
    all_to_all x1, blocking collectives, shards(): near = lax.all_to_all(sent, 'y', 0, 0, tiled=True)  15.1 us
    all_to_all x1, blocking collectives, finished(): return (mixed, scaled, lax.all_to_all(squares, 'tensor', 0, 0, tiled=True))  13.8 us
    ppermute x1, starting transfers between devices, swapped(): lax.ppermute(t, Z, [(first, first + 1), (first + 1, first)])  4.13 us
    ppermute x1, starting transfers between devices, shards(): halo = lax.ppermute(tails, CONTEXT, [(i, i + 1) for i in range(63)])  4.03 us
    pallas_call x1, Pallas kernels, shards(): call(local_part, 'local_part', [(whole, f32)] * 2 + [(modes, f32)] + [(ta...  2.77 us
    pallas_call x1, Pallas kernels, shards(): call(normalise, 'normalise', [(natural, bf16)] * 2, [vmem(natural, bf16),...  1.68 us
    pallas_call x1, Pallas kernels, finished(): call(body, body.__name__, results, [vmem(modes, f32), vmem((16 * GROUPS,...  1.57 us
    ppermute x1, waiting for transfers between devices, swapped(): lax.ppermute(t, Z, [(first, first + 1), (first + 1, first)])  1.39 us
  transfers between devices with their start and end apart: 5, of which 2 were waited for; matrix products, arithmetic and copies ran while one was open for 2% of the time, Pallas kernels for 9%

profile of v4, /device:TPU:1, one launch (start us, length us, event | category | flops | bytes accessed | tf_op | source)
XLA Modules:
  0.0 53.3 jit_solution(16412045971118674234)
XLA Ops:
  0.7 1.3 %fetch.1 = (bf16[24,1024]{1,0:T(8,128)(2,1)S(1)}, bf16[128,1024]{1,0:T(8,128)(2,1)S(1)}, bf16[128,1024]{1,0:T(8,128)(2,1)S(1)}, bf16[128,1024]{1,0:T(8,128)(2,1)S(1)}) custom-call(bf16[128,1024]{1,0:T(8,128)(2,1)} %q_hbm.1, bf16[128,1024]{1,0:T(8,128)(2,1)} %k_hbm.1, bf16[128,1024]{1,0:T(8,128)(2,1)} %v_hbm.1), custom_call_target="tpu_custom_call" | custom-call | tf_op jit(solution)/shard_map/fetch/pallas_call | solution.py:293
  1.9 4.0 %collective-permute-start.3 = (bf16[24,1024]{1,0:T(8,128)(2,1)S(1)}, bf16[24,1024]{1,0:T(8,128)(2,1)S(1)}, u32[]{:S(2)}, u32[]{:S(2)}) collective-permute-start(bf16[24,1024]{1,0:T(8,128)(2,1)S(1)} %get-tuple-element.168), channel_id=1, source_target_pairs={{0,8},{8,16},{16,24},{24,32},{32,40},{40,48},{48,56},{56,64},{64,7... | collective-permute-start | bytes 147464 | tf_op jit(solution)/shard_map/ppermute | solution.py:297
  6.0 0.1 pad_add_fusion.at_ref
  6.1 0.7 %copy-done.4 = f32[1024]{0:T(1024)S(1)} copy-done((f32[1024]{0:T(1024)S(1)}, f32[1024]{0:T(1024)}, u32[]{:S(2)}) %copy-start.4) | copy-done | bytes 4120
  6.8 2.8 %local_part.1 = (f32[1024,128]{1,0:T(8,128)S(1)}, f32[1024,128]{1,0:T(8,128)S(1)}, f32[128,128]{1,0:T(8,128)S(1)}, f32[192,128]{1,0:T(8,128)S(1)}, f32[192,128]{...) custom-call(s32[3]{0:T(128)S(1)} %pad_add_fusion.at_ref, ...), custom_call_target="tpu_custom_call" | custom-call | tf_op jit(solution)/shard_map/local_part/pallas_call | solution.py:298
  9.5 0.1 edge_part.1
  9.6 15.1 %all_to_all.39 = bf16[8,128,128]{2,1,0:T(8,128)(2,1)S(1)} all-to-all(bf16[8,128,128]{2,1,0:T(8,128)(2,1)S(1)} %bitcast.18), channel_id=1, replica_groups=mesh['half'=2,'place'=4,'y'=8,'tensor'=8] {'y'}, dimensions={0} | all-to-all | bytes 524288 | tf_op jit(solution)/shard_map/all_to_all | solution.py:307
  24.8 0.6 %scan_near.1 = (bf16[512,128]{1,0:T(8,128)(2,1)S(1)}, bf16[128,128]{1,0:T(8,128)(2,1)S(1)}, f32[128,128]{1,0:T(8,128)S(1)}, f32[128,128]{1,0:T(8,128)S(1)}) custom-call(s32[3]{0:T(128)S(1)} %pad_add_fusion.at_ref, bf16[1024,128]{1,0:T(8,128)(2,1)S(1)} %bitcast.17, f32[128,128]{1,0:T(8,128)S(1)} %get-tuple-element.174.dt), custom_call_target="tpu_custom_call" | custom-call | tf_op jit(solution)/shard_map/scan_near/pallas_call | solution.py:308
  25.4 8.7 %conditional.8 = ((bf16[128,128]{1,0:T(8,128)(2,1)S(1)}, f32[128,128]{1,0:T(8,128)S(1)})) conditional(s32[]{:T(128)} %convert_element_type.37, bf16[128,128]{1,0:T(8,128)(2,1)S(1)} %get-tuple-element.180, (f32[128,128]{1,0:T(8,128)S(1)}, s32[]{:T(128)}, bf16[128,128]{1,0:T(8,128)(2,1)S(1)}) %tuple.59), branch_computations={%region_0.0_spmd, %region_1.6_spmd} | conditional | flops 344073 | bytes 819448 | solution.py:335
  25.4 5.6 %conditional.3 = (bf16[128,128]{1,0:T(8,128)(2,1)}) conditional(s32[]{:T(128)} %convert_element_type.29, bf16[128,128]{1,0:T(8,128)(2,1)S(1)} %get-tuple-element.99, bf16[128,128]{1,0:T(8,128)(2,1)S(1)} %get-tuple-element.99), branch_computations={%region_2.0_spmd, %region_3.0_spmd} | conditional | bytes 131120 | solution.py:323
  25.5 4.1 %collective-permute-start = (bf16[128,128]{1,0:T(8,128)(2,1)S(1)}, bf16[128,128]{1,0:T(8,128)(2,1)}, u32[]{:S(2)}, u32[]{:S(2)}) collective-permute-start(bf16[128,128]{1,0:T(8,128)(2,1)S(1)} %param.2), channel_id=1, source_target_pairs={{0,64},{64,0},{1,65},{65,1},{2,66},{66,2},{3,67},{67,3},{4,68},{68... | collective-permute-start | bytes 98312 | tf_op jit(solution)/shard_map/cond/branch_1_fun/cond/branch_1_fun/ppermute | solution.py:316
  29.6 1.4 %collective-permute-done = bf16[128,128]{1,0:T(8,128)(2,1)} collective-permute-done((bf16[128,128]{1,0:T(8,128)(2,1)S(1)}, bf16[128,128]{1,0:T(8,128)(2,1)}, u32[]{:S(2)}, u32[]{:S(2)}) %collective-permute-start) | collective-permute-done | bytes 32800 | tf_op jit(solution)/shard_map/cond/branch_1_fun/cond/branch_1_fun/ppermute | solution.py:316
  31.0 0.8 %fusion.2 = bf16[128,128]{1,0:T(8,128)(2,1)S(1)} fusion(f32[128,128]{1,0:T(8,128)S(1)} %get-tuple-element.96, bf16[128,128]{1,0:T(8,128)(2,1)} %get-tuple-element.221, bf16[128,128]{1,0:T(8,128)(2,1)S(1)} %get-tuple-element.99, pred[]{:T(512)S(6)} %eq.3), kind=kLoop, calls=%fused_computation.10 | loop fusion | flops 114688 | bytes 163841 | tf_op jit(solution)/shard_map/cond/branch_1_fun/convert_element_type | solution.py:324
  31.8 1.3 %collective-permute-start.2 = (bf16[128,128]{1,0:T(8,128)(2,1)S(1)}, bf16[128,128]{1,0:T(8,128)(2,1)S(1)}, u32[]{:S(2)}, u32[]{:S(2)}) collective-permute-start(bf16[128,128]{1,0:T(8,128)(2,1)S(1)} %fusion.2), channel_id=1, source_target_pairs={{0,128},{64,192},{1,129},{65,193},{2,130},{66,194},{3,131},{67,195... | collective-permute-start | bytes 98312 | tf_op jit(solution)/shard_map/cond/branch_1_fun/ppermute | solution.py:325
  33.1 0.8 %conditional.4 = (bf16[128,128]{1,0:T(8,128)(2,1)S(1)}) conditional(s32[]{:T(128)} %convert_element_type.29, bf16[128,128]{1,0:T(8,128)(2,1)S(1)} %get-tuple-element.99, bf16[128,128]{1,0:T(8,128)(2,1)} %get-tuple-element.221), branch_computations={%region_4.4_spmd, %region_5.5_spmd} | conditional | bytes 131120
  33.1 0.8 %copy.16 = bf16[128,128]{1,0:T(8,128)(2,1)S(1)} copy(bf16[128,128]{1,0:T(8,128)(2,1)} %param.4) | data formatting | bytes 65536 | tf_op jit(solution)/shard_map/conditional.1
  33.9 0.2 collective-permute-done.2
  34.1 0.7 %collective-permute-start.4 = (bf16[128,128]{1,0:T(8,128)(2,1)S(1)}, bf16[128,128]{1,0:T(8,128)(2,1)S(1)}, u32[]{:S(2)}, u32[]{:S(2)}) collective-permute-start(bf16[128,128]{1,0:T(8,128)(2,1)S(1)} %get-tuple-element.182), channel_id=1, source_target_pairs={{128,384},{192,448},{129,385},{193,449},{130,386},{194,450},{131,3... | collective-permute-start | bytes 98312 | tf_op jit(solution)/shard_map/ppermute | solution.py:336
  34.8 0.7 %collective-permute-start.5 = (bf16[128,128]{1,0:T(8,128)(2,1)S(1)}, bf16[128,128]{1,0:T(8,128)(2,1)S(1)}, u32[]{:S(2)}, u32[]{:S(2)}) collective-permute-start(bf16[128,128]{1,0:T(8,128)(2,1)S(1)} %get-tuple-element.182), channel_id=1, source_target_pairs={{128,256},{192,320},{129,257},{193,321},{130,258},{194,322},{131,2... | collective-permute-start | bytes 98312 | tf_op jit(solution)/shard_map/ppermute | solution.py:336
  35.5 16.1 %conditional.9 = (bf16[128,1024]{1,0:T(8,128)(2,1)S(1)}, f32[128,1024]{1,0:T(8,128)S(1)}, f32[8,128]{1,0:T(8,128)}, bf16[512,128]{1,0:T(8,128)(2,1)S(1)}) conditional(s32[]{:T(128)} %convert_element_type.37, bf16[512,128]{1,0:T(8,128)(2,1)S(1)} %get-tuple-element.185, (s32[3]{0:T(128)S(1)}, f32[128,128]{1,0:T(8,128)S(1)}, f32[128,128]{1,0:T(8,128)S(1)}, ...), branch_computations={%region_6.7_spmd, %region_7.8_spmd} | conditional | bytes 262176 | solution.py:356
  35.5 1.6 %finish_lower.1 = (bf16[128,1024]{1,0:T(8,128)(2,1)S(1)}, f32[128,1024]{1,0:T(8,128)S(1)}, f32[8,128]{1,0:T(8,128)S(1)}) custom-call(s32[3]{0:T(128)S(1)} %get-tuple-element.103.at_ref, f32[128,128]{1,0:T(8,128)S(1)} %get-tuple-element.104.far_ref, f32[128,128]{1,0:T(8,128)S(1)} %get-tuple-element.105.before_ref, f32[128,128]{1,0:T(8,128)S(1)} %get-tuple-element.106.dt, ...), custom_call_target="tpu_custom_call" | custom-call | tf_op jit(solution)/shard_map/cond/branch_1_fun/finish_lower/pallas_call | solution.py:341
  37.1 13.8 %all_to_all.37 = f32[8,1,128]{2,1,0:T(1,128)} all-to-all(f32[8,1,128]{2,1,0:T(1,128)S(1)} %bitcast.22), channel_id=1, replica_groups=mesh['half'=2,'place'=4,'y'=8,'tensor'=8] {'tensor'}, dimensions={0} | all-to-all | bytes 8192 | tf_op jit(solution)/shard_map/cond/branch_1_fun/all_to_all | solution.py:346
  50.9 0.7 %unwritten.5 = bf16[512,128]{1,0:T(8,128)(2,1)S(1)} custom-call(f32[8,128]{1,0:T(8,128)} %bitcast.4.__0_), custom_call_target="tpu_custom_call" | custom-call | tf_op jit(solution)/shard_map/cond/branch_1_fun/unwritten/pallas_call | solution.py:333
  51.6 1.7 %normalise.1 = (bf16[128,1024]{1,0:T(8,128)(2,1)}, bf16[128,1024]{1,0:T(8,128)(2,1)}) custom-call(bf16[128,1024]{1,0:T(8,128)(2,1)S(1)} %get-tuple-element.198.mixed_ref, f32[128,1024]{1,0:T(8,128)S(1)} %get-tuple-element.199.scaled_ref, f32[8,128]{1,0:T(8,128)} %get-tuple-element.200.squares_ref), custom_call_target="tpu_custom_call" | custom-call | tf_op jit(solution)/shard_map/normalise/pallas_call | solution.py:361
  (16 shorter events, 0.1 us)
Async XLA Ops:
  0.6 5.4 %copy-start = (f32[3,7,1024]{2,1,0:T(8,128)S(1)}, f32[3,7,1024]{2,1,0:T(8,128)}, u32[]{:S(2)}) copy-start(f32[3,7,1024]{2,1,0:T(8,128)} %f_ref.1) | copy-start | bytes 258052
  0.6 5.4 %copy-start.1 = (f32[16,1024]{1,0:T(8,128)S(1)}, f32[16,1024]{1,0:T(8,128)}, u32[]{:S(2)}) copy-start(f32[16,1024]{1,0:T(8,128)} %d_ref.1) | copy-start | bytes 196612
  0.7 5.4 %copy-start.2 = (f32[16,1024]{1,0:T(8,128)S(1)}, f32[16,1024]{1,0:T(8,128)}, u32[]{:S(2)}) copy-start(f32[16,1024]{1,0:T(8,128)} %r_ref.1) | copy-start | bytes 196612
  1.9 7.6 %collective-permute-start.3 = (bf16[24,1024]{1,0:T(8,128)(2,1)S(1)}, bf16[24,1024]{1,0:T(8,128)(2,1)S(1)}, u32[]{:S(2)}, u32[]{:S(2)}) collective-permute-start(bf16[24,1024]{1,0:T(8,128)(2,1)S(1)} %get-tuple-element.168), channel_id=1, source_target_pairs={{0,8},{8,16},{16,24},{24,32},{32,40},{40,48},{48,56},{56,64},{64,7... | collective-permute-start | bytes 147464 | tf_op jit(solution)/shard_map/ppermute | solution.py:297
  6.0 0.7 %copy-start.4 = (f32[1024]{0:T(1024)S(1)}, f32[1024]{0:T(1024)}, u32[]{:S(2)}) copy-start(f32[1024]{0:T(1024)} %param.27) | copy-start | bytes 12292
  6.0 0.7 %copy-start.3 = (f32[1024]{0:T(1024)S(1)}, f32[1024]{0:T(1024)}, u32[]{:S(2)}) copy-start(f32[1024]{0:T(1024)} %param.25) | copy-start | bytes 12292
  25.4 10.1 %copy-start.5 = (bf16[128,1024]{1,0:T(8,128)(2,1)S(1)}, bf16[128,1024]{1,0:T(8,128)(2,1)}, u32[]{:S(2)}) copy-start(bf16[128,1024]{1,0:T(8,128)(2,1)} %param.26) | copy-start | bytes 786436
  25.5 5.5 %collective-permute-start = (bf16[128,128]{1,0:T(8,128)(2,1)S(1)}, bf16[128,128]{1,0:T(8,128)(2,1)}, u32[]{:S(2)}, u32[]{:S(2)}) collective-permute-start(bf16[128,128]{1,0:T(8,128)(2,1)S(1)} %param.2), channel_id=1, source_target_pairs={{0,64},{64,0},{1,65},{65,1},{2,66},{66,2},{3,67},{67,3},{4,68},{68... | collective-permute-start | bytes 98312 | tf_op jit(solution)/shard_map/cond/branch_1_fun/cond/branch_1_fun/ppermute | solution.py:316
  31.8 2.3 %collective-permute-start.2 = (bf16[128,128]{1,0:T(8,128)(2,1)S(1)}, bf16[128,128]{1,0:T(8,128)(2,1)S(1)}, u32[]{:S(2)}, u32[]{:S(2)}) collective-permute-start(bf16[128,128]{1,0:T(8,128)(2,1)S(1)} %fusion.2), channel_id=1, source_target_pairs={{0,128},{64,192},{1,129},{65,193},{2,130},{66,194},{3,131},{67,195... | collective-permute-start | bytes 98312 | tf_op jit(solution)/shard_map/cond/branch_1_fun/ppermute | solution.py:325
  34.1 17.5 %collective-permute-start.4 = (bf16[128,128]{1,0:T(8,128)(2,1)S(1)}, bf16[128,128]{1,0:T(8,128)(2,1)S(1)}, u32[]{:S(2)}, u32[]{:S(2)}) collective-permute-start(bf16[128,128]{1,0:T(8,128)(2,1)S(1)} %get-tuple-element.182), channel_id=1, source_target_pairs={{128,384},{192,448},{129,385},{193,449},{130,386},{194,450},{131,3... | collective-permute-start | bytes 98312 | tf_op jit(solution)/shard_map/ppermute | solution.py:336
  34.8 16.8 %collective-permute-start.5 = (bf16[128,128]{1,0:T(8,128)(2,1)S(1)}, bf16[128,128]{1,0:T(8,128)(2,1)S(1)}, u32[]{:S(2)}, u32[]{:S(2)}) collective-permute-start(bf16[128,128]{1,0:T(8,128)(2,1)S(1)} %get-tuple-element.182), channel_id=1, source_target_pairs={{128,256},{192,320},{129,257},{193,321},{130,258},{194,322},{131,2... | collective-permute-start | bytes 98312 | tf_op jit(solution)/shard_map/ppermute | solution.py:336

commit v5 on v4

--- a/solution.py
+++ b/solution.py
@@ -338,16 +338,15 @@
     results = (natural, bf16), (natural, f32), ((8, LANES), f32)
 
     def finished(body, count, *own_args):
-        mixed, scaled, squares = call(
+        return call(
             body, body.__name__, results,
             [vmem(modes, f32), vmem((16 * GROUPS, LANES), f32), vmem((ROWS, LANES), f32)],
             count, 1,
         )(at, *own_args, before, rates, weights, skip, qc, own, edge, residual, gain)
-        return mixed, scaled, lax.all_to_all(squares, "tensor", 0, 0, tiled=True)
 
     def lower(_):
         done = finished(finish_lower, 11, far)
-        return *done, *unwritten(done[2], (quads, bf16))
+        return *done, *unwritten(far, (quads, bf16))
 
     def upper(_):
         quad = lax.all_to_all(quads_out, "place", 0, 0, tiled=True)
@@ -355,9 +354,10 @@
 
     *done, quad = lax.cond(z < 4, lower, upper, 0)
     carried = carried[0] + carried[1]
-    mixed, scaled, gathered = lax.cond(
+    mixed, scaled, squares = lax.cond(
         z < 4, lambda d: d, lambda _: finished(finish_upper, 12, quad, carried), tuple(done)
     )
+    gathered = lax.all_to_all(squares, "tensor", 0, 0, tiled=True)
     return call(
         normalise, "normalise", [(natural, bf16)] * 2, [vmem(natural, bf16), pltpu.SemaphoreType.DMA((3,))],
         3, far_out=True,

time: 54.1 us -> 53.2 us (0.983)
  the two profiles are of different devices: /device:TPU:1 before, /device:TPU:320 now
where the time goes in v5:
time: 53.2 us; the launch traced here: 52.8 us
  blocking collectives  36.2 us (68%)
  Pallas kernels  7.36 us (14%)
  starting transfers between devices  5.57 us (10%)
  waiting for transfers between devices  2.08 us (4%)
  between operations  0.76 us (1%)
  local copies, waits for them, and re-layouts  0.7 us (1%)
    all_to_all x1, blocking collectives, shards(): near = lax.all_to_all(sent, 'y', 0, 0, tiled=True)  16.7 us
    all_to_all x1, blocking collectives, upper(): quad = lax.all_to_all(quads_out, 'place', 0, 0, tiled=True)  10.1 us
    all_to_all x1, blocking collectives, shards(): gathered = lax.all_to_all(squares, 'tensor', 0, 0, tiled=True)  9.38 us
    ppermute x1, starting transfers between devices, shards(): halo = lax.ppermute(tails, CONTEXT, [(i, i + 1) for i in range(63)])  3.48 us
    pallas_call x1, Pallas kernels, shards(): call(local_part, 'local_part', [(whole, f32)] * 2 + [(modes, f32)] + [(ta...  2.77 us
    pallas_call x1, Pallas kernels, finished(): call(body, body.__name__, results, [vmem(modes, f32), vmem((16 * GROUPS,...  1.61 us
    ppermute x1, starting transfers between devices, shards(): lax.ppermute(four, Z, [(2, 4), (3, 5)])  1.29 us
    pallas_call x1, Pallas kernels, shards(): call(fetch, 'fetch', [((24, natural[1]), bf16)] + [(natural, bf16)] * 3,...  1.26 us
  transfers between devices with their start and end apart: 3, of which 2 were waited for; matrix products, arithmetic and copies ran while one was open for 0% of the time, Pallas kernels for 5%

profile of v5, /device:TPU:320, one launch (start us, length us, event | category | flops | bytes accessed | tf_op | source)
XLA Modules:
  0.0 52.8 jit_solution(2254264550899565241)
XLA Ops:
  0.6 0.0 copy-start
  0.6 0.0 copy-start.1
  0.7 0.0 copy-start.2
  0.7 1.3 %fetch.1 = (bf16[24,1024]{1,0:T(8,128)(2,1)S(1)}, bf16[128,1024]{1,0:T(8,128)(2,1)S(1)}, bf16[128,1024]{1,0:T(8,128)(2,1)S(1)}, bf16[128,1024]{1,0:T(8,128)(2,1)S(1)}) custom-call(bf16[128,1024]{1,0:T(8,128)(2,1)} %q_hbm.1, bf16[128,1024]{1,0:T(8,128)(2,1)} %k_hbm.1, bf16[128,1024]{1,0:T(8,128)(2,1)} %v_hbm.1), custom_call_target="tpu_custom_call" | custom-call | tf_op jit(solution)/shard_map/fetch/pallas_call | solution.py:293
  1.9 3.5 %collective-permute-start.3 = (bf16[24,1024]{1,0:T(8,128)(2,1)S(1)}, bf16[24,1024]{1,0:T(8,128)(2,1)S(1)}, u32[]{:S(2)}, u32[]{:S(2)}) collective-permute-start(bf16[24,1024]{1,0:T(8,128)(2,1)S(1)} %get-tuple-element.165), channel_id=1, source_target_pairs={{0,8},{8,16},{16,24},{24,32},{32,40},{40,48},{48,56},{56,64},{64,7... | collective-permute-start | bytes 147464 | tf_op jit(solution)/shard_map/ppermute | solution.py:297
  5.4 0.1 pad_add_fusion.at_ref
  5.5 0.7 %copy-done.4 = f32[1024]{0:T(1024)S(1)} copy-done((f32[1024]{0:T(1024)S(1)}, f32[1024]{0:T(1024)}, u32[]{:S(2)}) %copy-start.4) | copy-done | bytes 4120
  6.2 0.0 copy-done.3
  6.2 2.8 %local_part.1 = (f32[1024,128]{1,0:T(8,128)S(1)}, f32[1024,128]{1,0:T(8,128)S(1)}, f32[128,128]{1,0:T(8,128)S(1)}, f32[192,128]{1,0:T(8,128)S(1)}, f32[192,128]{...) custom-call(s32[3]{0:T(128)S(1)} %pad_add_fusion.at_ref, ...), custom_call_target="tpu_custom_call" | custom-call | tf_op jit(solution)/shard_map/local_part/pallas_call | solution.py:298
  9.0 1.0 %collective-permute-done.3.halo_ref = bf16[24,1024]{1,0:T(8,128)(2,1)S(1)} collective-permute-done((bf16[24,1024]{1,0:T(8,128)(2,1)S(1)}, bf16[24,1024]{1,0:T(8,128)(2,1)S(1)}, u32[]{:S(2)}, u32[]{:S(2)}) %collective-permute-start.3) | collective-permute-done | bytes 49184 | tf_op jit(solution)/shard_map/ppermute | solution.py:297
  10.0 0.1 edge_part.1
  10.1 16.7 %all_to_all.31 = bf16[8,128,128]{2,1,0:T(8,128)(2,1)S(1)} all-to-all(bf16[8,128,128]{2,1,0:T(8,128)(2,1)S(1)} %bitcast.12), channel_id=1, replica_groups=mesh['half'=2,'place'=4,'y'=8,'tensor'=8] {'y'}, dimensions={0} | all-to-all | bytes 524288 | tf_op jit(solution)/shard_map/all_to_all | solution.py:307
  26.8 0.6 %scan_near.1 = (bf16[512,128]{1,0:T(8,128)(2,1)S(1)}, bf16[128,128]{1,0:T(8,128)(2,1)S(1)}, f32[128,128]{1,0:T(8,128)S(1)}, f32[128,128]{1,0:T(8,128)S(1)}) custom-call(s32[3]{0:T(128)S(1)} %pad_add_fusion.at_ref, bf16[1024,128]{1,0:T(8,128)(2,1)S(1)} %bitcast.11, f32[128,128]{1,0:T(8,128)S(1)} %get-tuple-element.171.dt), custom_call_target="tpu_custom_call" | custom-call | tf_op jit(solution)/shard_map/scan_near/pallas_call | solution.py:308
  27.5 0.0 copy-start.5
  27.5 0.8 %collective-permute-start.4 = (bf16[128,128]{1,0:T(8,128)(2,1)S(1)}, bf16[128,128]{1,0:T(8,128)(2,1)S(1)}, u32[]{:S(2)}, u32[]{:S(2)}) collective-permute-start(bf16[128,128]{1,0:T(8,128)(2,1)S(1)} %get-tuple-element.179), channel_id=1, source_target_pairs={{128,384},{192,448},{129,385},{193,449},{130,386},{194,450},{131,3... | collective-permute-start | bytes 98312 | tf_op jit(solution)/shard_map/ppermute | solution.py:336
  28.3 1.3 %collective-permute-start.5 = (bf16[128,128]{1,0:T(8,128)(2,1)S(1)}, bf16[128,128]{1,0:T(8,128)(2,1)S(1)}, u32[]{:S(2)}, u32[]{:S(2)}) collective-permute-start(bf16[128,128]{1,0:T(8,128)(2,1)S(1)} %get-tuple-element.179), channel_id=1, source_target_pairs={{128,256},{192,320},{129,257},{193,321},{130,258},{194,322},{131,2... | collective-permute-start | bytes 98312 | tf_op jit(solution)/shard_map/ppermute | solution.py:336
  29.6 10.1 %conditional.9 = (bf16[128,1024]{1,0:T(8,128)(2,1)S(1)}, f32[128,1024]{1,0:T(8,128)S(1)}, f32[8,128]{1,0:T(8,128)S(1)}, bf16[512,128]{1,0:T(8,128)(2,1)S(1)}) conditional(s32[]{:T(128)} %convert_element_type.37, bf16[512,128]{1,0:T(8,128)(2,1)S(1)} %get-tuple-element.182, (s32[3]{0:T(128)S(1)}, f32[128,128]{1,0:T(8,128)S(1)}, ...), branch_computations={%region_6.7_spmd, %region_7.8_spmd} | conditional | bytes 262176 | solution.py:355
  29.7 10.1 %all_to_all.30 = bf16[4,128,128]{2,1,0:T(8,128)(2,1)S(1)} all-to-all(bf16[4,128,128]{2,1,0:T(8,128)(2,1)S(1)} %bitcast.18), channel_id=1, replica_groups=mesh['half'=2,'place'=4,'y'=8,'tensor'=8] {'place'}, dimensions={0} | all-to-all | bytes 262144 | tf_op jit(solution)/shard_map/cond/branch_0_fun/all_to_all | solution.py:352
  39.7 0.0 collective-permute-done.4
  39.7 1.0 %collective-permute-done.5 = bf16[128,128]{1,0:T(8,128)(2,1)S(1)} collective-permute-done((bf16[128,128]{1,0:T(8,128)(2,1)S(1)}, bf16[128,128]{1,0:T(8,128)(2,1)S(1)}, u32[]{:S(2)}, u32[]{:S(2)}) %collective-permute-start.5) | collective-permute-done | bytes 32800 | tf_op jit(solution)/shard_map/ppermute | solution.py:336
  40.8 1.6 %conditional.10 = ((bf16[128,1024]{1,0:T(8,128)(2,1)S(1)}, f32[128,1024]{1,0:T(8,128)S(1)}, f32[8,128]{1,0:T(8,128)S(1)})) conditional(s32[]{:T(128)} %convert_element_type.37, (bf16[128,128]{1,0:T(8,128)(2,1)S(1)}, bf16[128,128]{1,0:T(8,128)(2,1)S(1)}, s32[3]{0:T(128)S(1)}, bf16[512,128]{1,0:T(8,128)(2,1)S(1)}, f32[128,128]{1,0:T(8,128)S(1)}, ...), branch_computations={%region_8.9_spmd, %region_9.10_spmd} | conditional | flops 16384 | bytes 98312 | solution.py:357
  40.8 1.6 %finish_upper.1 = (bf16[128,1024]{1,0:T(8,128)(2,1)S(1)}, f32[128,1024]{1,0:T(8,128)S(1)}, f32[8,128]{1,0:T(8,128)S(1)}) custom-call(s32[3]{0:T(128)S(1)} %get-tuple-element.117.at_ref, bf16[512,128]{1,0:T(8,128)(2,1)S(1)} %get-tuple-element.118.got_ref, bf16[128,128]{1,0:T(8,128)(2,1)S(1)} %add.17.half_ref, f32[128,128]{1,0:T(8,128)S(1)} %get-tuple-element.121.before_ref, ...), custom_call_target="tpu_custom_call" | custom-call | tf_op jit(solution)/shard_map/cond/branch_0_fun/finish_upper/pallas_call | solution.py:341
  42.4 9.4 %all_to_all.32 = f32[8,1,128]{2,1,0:T(1,128)S(1)} all-to-all(f32[8,1,128]{2,1,0:T(1,128)S(1)} %bitcast.19), channel_id=1, replica_groups=mesh['half'=2,'place'=4,'y'=8,'tensor'=8] {'tensor'}, dimensions={0} | all-to-all | bytes 8192 | tf_op jit(solution)/shard_map/all_to_all | solution.py:360
  51.8 1.0 %normalise.1 = (bf16[128,1024]{1,0:T(8,128)(2,1)}, bf16[128,1024]{1,0:T(8,128)(2,1)}) custom-call(bf16[128,1024]{1,0:T(8,128)(2,1)S(1)} %get-tuple-element.195.mixed_ref, f32[128,1024]{1,0:T(8,128)S(1)} %get-tuple-element.196.scaled_ref, f32[8,128]{1,0:T(8,128)S(1)} %bitcast.13), custom_call_target="tpu_custom_call" | custom-call | tf_op jit(solution)/shard_map/normalise/pallas_call | solution.py:361
  (10 shorter events, 0.0 us)
Async XLA Ops:
  0.6 4.9 %copy-start = (f32[3,7,1024]{2,1,0:T(8,128)S(1)}, f32[3,7,1024]{2,1,0:T(8,128)}, u32[]{:S(2)}) copy-start(f32[3,7,1024]{2,1,0:T(8,128)} %f_ref.1) | copy-start | bytes 258052
  0.6 4.9 %copy-start.1 = (f32[16,1024]{1,0:T(8,128)S(1)}, f32[16,1024]{1,0:T(8,128)}, u32[]{:S(2)}) copy-start(f32[16,1024]{1,0:T(8,128)} %d_ref.1) | copy-start | bytes 196612
  0.7 4.9 %copy-start.2 = (f32[16,1024]{1,0:T(8,128)S(1)}, f32[16,1024]{1,0:T(8,128)}, u32[]{:S(2)}) copy-start(f32[16,1024]{1,0:T(8,128)} %r_ref.1) | copy-start | bytes 196612
  1.9 8.1 %collective-permute-start.3 = (bf16[24,1024]{1,0:T(8,128)(2,1)S(1)}, bf16[24,1024]{1,0:T(8,128)(2,1)S(1)}, u32[]{:S(2)}, u32[]{:S(2)}) collective-permute-start(bf16[24,1024]{1,0:T(8,128)(2,1)S(1)} %get-tuple-element.165), channel_id=1, source_target_pairs={{0,8},{8,16},{16,24},{24,32},{32,40},{40,48},{48,56},{56,64},{64,7... | collective-permute-start | bytes 147464 | tf_op jit(solution)/shard_map/ppermute | solution.py:297
  5.5 0.7 %copy-start.4 = (f32[1024]{0:T(1024)S(1)}, f32[1024]{0:T(1024)}, u32[]{:S(2)}) copy-start(f32[1024]{0:T(1024)} %param.27) | copy-start | bytes 12292
  5.5 0.7 %copy-start.3 = (f32[1024]{0:T(1024)S(1)}, f32[1024]{0:T(1024)}, u32[]{:S(2)}) copy-start(f32[1024]{0:T(1024)} %param.25) | copy-start | bytes 12292
  27.5 2.1 %copy-start.5 = (bf16[128,1024]{1,0:T(8,128)(2,1)S(1)}, bf16[128,1024]{1,0:T(8,128)(2,1)}, u32[]{:S(2)}) copy-start(bf16[128,1024]{1,0:T(8,128)(2,1)} %param.26) | copy-start | bytes 786436
  27.5 12.2 %collective-permute-start.4 = (bf16[128,128]{1,0:T(8,128)(2,1)S(1)}, bf16[128,128]{1,0:T(8,128)(2,1)S(1)}, u32[]{:S(2)}, u32[]{:S(2)}) collective-permute-start(bf16[128,128]{1,0:T(8,128)(2,1)S(1)} %get-tuple-element.179), channel_id=1, source_target_pairs={{128,384},{192,448},{129,385},{193,449},{130,386},{194,450},{131,3... | collective-permute-start | bytes 98312 | tf_op jit(solution)/shard_map/ppermute | solution.py:336
  28.3 12.4 %collective-permute-start.5 = (bf16[128,128]{1,0:T(8,128)(2,1)S(1)}, bf16[128,128]{1,0:T(8,128)(2,1)S(1)}, u32[]{:S(2)}, u32[]{:S(2)}) collective-permute-start(bf16[128,128]{1,0:T(8,128)(2,1)S(1)} %get-tuple-element.179), channel_id=1, source_target_pairs={{128,256},{192,320},{129,257},{193,321},{130,258},{194,322},{131,2... | collective-permute-start | bytes 98312 | tf_op jit(solution)/shard_map/ppermute | solution.py:336

commit v6 on v5

--- a/solution.py
+++ b/solution.py
@@ -313,21 +313,21 @@
     even = lax.rem(z, 2) == 0
 
     def swapped(first):
-        return lambda t, _: lax.ppermute(t, Z, [(first, first + 1), (first + 1, first)])
+        return lambda t, _: lax.ppermute(t, Z, [(first, first + 1), (first + 1, first)]).astype(f32)
 
     def summed(mine, other):
-        mine, other = mine.astype(f32), other.astype(f32)
+        mine = mine.astype(f32)
         return step * jnp.where(even, mine, other) + jnp.where(even, other, mine)
 
     def by_pairs(total):
-        other = lax.cond(z < 2, swapped(0), lambda _, o: o, total, total)
+        other = lax.cond(z < 2, swapped(0), lambda _, o: o, total, step)
         pair = summed(total, other).astype(bf16)
         arrived = lax.ppermute(pair, Z, [(0, 2), (1, 3)])
         total, pair = lax.optimization_barrier((total, pair))
         other = lax.cond(z < 2, lambda _, o: o, swapped(2), total, other)
         arrived = arrived.astype(f32)
         four = (step * step * arrived + summed(total, other)).astype(bf16)
-        return four, jnp.where(even, arrived, step * arrived + other.astype(f32))
+        return four, jnp.where(even, arrived, step * arrived + other)
 
     def unwritten(after, *outs):
         return call(lambda *_: None, "unwritten", outs, [], 1)(after)

time: 53.2 us -> 52.3 us (0.983)
  the two profiles are of different devices: /device:TPU:320 before, /device:TPU:256 now
where the time goes in v6:
time: 52.3 us; the launch traced here: 52 us
  blocking collectives  35.2 us (67%)
  Pallas kernels  7.36 us (14%)
  starting transfers between devices  5.57 us (11%)
  waiting for transfers between devices  2.25 us (4%)
  between operations  0.77 us (1%)
  local copies, waits for them, and re-layouts  0.7 us (1%)
    all_to_all x1, blocking collectives, shards(): near = lax.all_to_all(sent, 'y', 0, 0, tiled=True)  15.5 us
    all_to_all x1, blocking collectives, upper(): quad = lax.all_to_all(quads_out, 'place', 0, 0, tiled=True)  10.3 us
    all_to_all x1, blocking collectives, shards(): gathered = lax.all_to_all(squares, 'tensor', 0, 0, tiled=True)  9.38 us
    ppermute x1, starting transfers between devices, shards(): halo = lax.ppermute(tails, CONTEXT, [(i, i + 1) for i in range(63)])  3.48 us
    pallas_call x1, Pallas kernels, shards(): call(local_part, 'local_part', [(whole, f32)] * 2 + [(modes, f32)] + [(ta...  2.77 us
    ppermute x1, waiting for transfers between devices, shards(): halo = lax.ppermute(tails, CONTEXT, [(i, i + 1) for i in range(63)])  2.25 us
    pallas_call x1, Pallas kernels, finished(): call(body, body.__name__, results, [vmem(modes, f32), vmem((16 * GROUPS,...  1.61 us
    ppermute x1, starting transfers between devices, shards(): lax.ppermute(four, Z, [(2, 4), (3, 5)])  1.29 us
  transfers between devices with their start and end apart: 3, of which 1 were waited for; matrix products, arithmetic and copies ran while one was open for 0% of the time, Pallas kernels for 5%

profile of v6, /device:TPU:256, one launch (start us, length us, event | category | flops | bytes accessed | tf_op | source)
XLA Modules:
  0.0 52.0 jit_solution(14022891580299374265)
XLA Ops:
  0.6 0.0 copy-start
  0.6 0.0 copy-start.1
  0.7 0.0 copy-start.2
  0.7 1.3 %fetch.1 = (bf16[24,1024]{1,0:T(8,128)(2,1)S(1)}, bf16[128,1024]{1,0:T(8,128)(2,1)S(1)}, bf16[128,1024]{1,0:T(8,128)(2,1)S(1)}, bf16[128,1024]{1,0:T(8,128)(2,1)S(1)}) custom-call(bf16[128,1024]{1,0:T(8,128)(2,1)} %q_hbm.1, bf16[128,1024]{1,0:T(8,128)(2,1)} %k_hbm.1, bf16[128,1024]{1,0:T(8,128)(2,1)} %v_hbm.1), custom_call_target="tpu_custom_call" | custom-call | tf_op jit(solution)/shard_map/fetch/pallas_call | solution.py:293
  1.9 3.5 %collective-permute-start.3 = (bf16[24,1024]{1,0:T(8,128)(2,1)S(1)}, bf16[24,1024]{1,0:T(8,128)(2,1)S(1)}, u32[]{:S(2)}, u32[]{:S(2)}) collective-permute-start(bf16[24,1024]{1,0:T(8,128)(2,1)S(1)} %get-tuple-element.157), channel_id=1, source_target_pairs={{0,8},{8,16},{16,24},{24,32},{32,40},{40,48},{48,56},{56,64},{64,7... | collective-permute-start | bytes 147464 | tf_op jit(solution)/shard_map/ppermute | solution.py:297
  5.4 0.1 pad_add_fusion.at_ref
  5.5 0.7 %copy-done.4 = f32[1024]{0:T(1024)S(1)} copy-done((f32[1024]{0:T(1024)S(1)}, f32[1024]{0:T(1024)}, u32[]{:S(2)}) %copy-start.4) | copy-done | bytes 4120
  6.2 0.0 copy-done.3
  6.2 2.8 %local_part.1 = (f32[1024,128]{1,0:T(8,128)S(1)}, f32[1024,128]{1,0:T(8,128)S(1)}, f32[128,128]{1,0:T(8,128)S(1)}, f32[192,128]{1,0:T(8,128)S(1)}, f32[192,128]{...) custom-call(s32[3]{0:T(128)S(1)} %pad_add_fusion.at_ref, ...), custom_call_target="tpu_custom_call" | custom-call | tf_op jit(solution)/shard_map/local_part/pallas_call | solution.py:298
  9.0 2.2 %collective-permute-done.3.halo_ref = bf16[24,1024]{1,0:T(8,128)(2,1)S(1)} collective-permute-done((bf16[24,1024]{1,0:T(8,128)(2,1)S(1)}, bf16[24,1024]{1,0:T(8,128)(2,1)S(1)}, u32[]{:S(2)}, u32[]{:S(2)}) %collective-permute-start.3) | collective-permute-done | bytes 49184 | tf_op jit(solution)/shard_map/ppermute | solution.py:297
  11.2 0.1 edge_part.1
  11.3 15.5 %all_to_all.31 = bf16[8,128,128]{2,1,0:T(8,128)(2,1)S(1)} all-to-all(bf16[8,128,128]{2,1,0:T(8,128)(2,1)S(1)} %bitcast.12), channel_id=1, replica_groups=mesh['half'=2,'place'=4,'y'=8,'tensor'=8] {'y'}, dimensions={0} | all-to-all | bytes 524288 | tf_op jit(solution)/shard_map/all_to_all | solution.py:307
  26.8 0.6 %scan_near.1 = (bf16[512,128]{1,0:T(8,128)(2,1)S(1)}, bf16[128,128]{1,0:T(8,128)(2,1)S(1)}, f32[128,128]{1,0:T(8,128)S(1)}, f32[128,128]{1,0:T(8,128)S(1)}) custom-call(s32[3]{0:T(128)S(1)} %pad_add_fusion.at_ref, bf16[1024,128]{1,0:T(8,128)(2,1)S(1)} %bitcast.11, f32[128,128]{1,0:T(8,128)S(1)} %get-tuple-element.163.dt), custom_call_target="tpu_custom_call" | custom-call | tf_op jit(solution)/shard_map/scan_near/pallas_call | solution.py:308
  27.5 0.0 copy-start.5
  27.5 0.8 %collective-permute-start.4 = (bf16[128,128]{1,0:T(8,128)(2,1)S(1)}, bf16[128,128]{1,0:T(8,128)(2,1)S(1)}, u32[]{:S(2)}, u32[]{:S(2)}) collective-permute-start(bf16[128,128]{1,0:T(8,128)(2,1)S(1)} %get-tuple-element.171), channel_id=1, source_target_pairs={{128,384},{192,448},{129,385},{193,449},{130,386},{194,450},{131,3... | collective-permute-start | bytes 98312 | tf_op jit(solution)/shard_map/ppermute | solution.py:336
  28.3 1.3 %collective-permute-start.5 = (bf16[128,128]{1,0:T(8,128)(2,1)S(1)}, bf16[128,128]{1,0:T(8,128)(2,1)S(1)}, u32[]{:S(2)}, u32[]{:S(2)}) collective-permute-start(bf16[128,128]{1,0:T(8,128)(2,1)S(1)} %get-tuple-element.171), channel_id=1, source_target_pairs={{128,256},{192,320},{129,257},{193,321},{130,258},{194,322},{131,2... | collective-permute-start | bytes 98312 | tf_op jit(solution)/shard_map/ppermute | solution.py:336
  29.6 10.3 %conditional.6 = (bf16[128,1024]{1,0:T(8,128)(2,1)S(1)}, f32[128,1024]{1,0:T(8,128)S(1)}, f32[8,128]{1,0:T(8,128)S(1)}, bf16[512,128]{1,0:T(8,128)(2,1)S(1)}) conditional(s32[]{:T(128)} %convert_element_type.30, bf16[512,128]{1,0:T(8,128)(2,1)S(1)} %get-tuple-element.174, (s32[3]{0:T(128)S(1)}, f32[128,128]{1,0:T(8,128)S(1)}, ...), branch_computations={%region_6.7_spmd, %region_7.8_spmd} | conditional | bytes 262176 | solution.py:355
  29.7 10.3 %all_to_all.30 = bf16[4,128,128]{2,1,0:T(8,128)(2,1)S(1)} all-to-all(bf16[4,128,128]{2,1,0:T(8,128)(2,1)S(1)} %bitcast.18), channel_id=1, replica_groups=mesh['half'=2,'place'=4,'y'=8,'tensor'=8] {'place'}, dimensions={0} | all-to-all | bytes 262144 | tf_op jit(solution)/shard_map/cond/branch_0_fun/all_to_all | solution.py:352
  39.9 0.0 collective-permute-done.4
  39.9 0.0 collective-permute-done.5
  40.0 1.6 %conditional.7 = ((bf16[128,1024]{1,0:T(8,128)(2,1)S(1)}, f32[128,1024]{1,0:T(8,128)S(1)}, f32[8,128]{1,0:T(8,128)S(1)})) conditional(s32[]{:T(128)} %convert_element_type.30, (bf16[128,128]{1,0:T(8,128)(2,1)S(1)}, bf16[128,128]{1,0:T(8,128)(2,1)S(1)}, s32[3]{0:T(128)S(1)}, bf16[512,128]{1,0:T(8,128)(2,1)S(1)}, f32[128,128]{1,0:T(8,128)S(1)}, ...), branch_computations={%region_8.9_spmd, %region_9.10_spmd} | conditional | flops 16384 | bytes 98312 | solution.py:357
  40.0 1.6 %finish_upper.1 = (bf16[128,1024]{1,0:T(8,128)(2,1)S(1)}, f32[128,1024]{1,0:T(8,128)S(1)}, f32[8,128]{1,0:T(8,128)S(1)}) custom-call(s32[3]{0:T(128)S(1)} %get-tuple-element.109.at_ref, bf16[512,128]{1,0:T(8,128)(2,1)S(1)} %get-tuple-element.110.got_ref, bf16[128,128]{1,0:T(8,128)(2,1)S(1)} %add.17.half_ref, f32[128,128]{1,0:T(8,128)S(1)} %get-tuple-element.113.before_ref, ...), custom_call_target="tpu_custom_call" | custom-call | tf_op jit(solution)/shard_map/cond/branch_0_fun/finish_upper/pallas_call | solution.py:341
  41.6 9.4 %all_to_all.32 = f32[8,1,128]{2,1,0:T(1,128)S(1)} all-to-all(f32[8,1,128]{2,1,0:T(1,128)S(1)} %bitcast.19), channel_id=1, replica_groups=mesh['half'=2,'place'=4,'y'=8,'tensor'=8] {'tensor'}, dimensions={0} | all-to-all | bytes 8192 | tf_op jit(solution)/shard_map/all_to_all | solution.py:360
  51.0 1.0 %normalise.1 = (bf16[128,1024]{1,0:T(8,128)(2,1)}, bf16[128,1024]{1,0:T(8,128)(2,1)}) custom-call(bf16[128,1024]{1,0:T(8,128)(2,1)S(1)} %get-tuple-element.187.mixed_ref, f32[128,1024]{1,0:T(8,128)S(1)} %get-tuple-element.188.scaled_ref, f32[8,128]{1,0:T(8,128)S(1)} %bitcast.13), custom_call_target="tpu_custom_call" | custom-call | tf_op jit(solution)/shard_map/normalise/pallas_call | solution.py:361
  (10 shorter events, 0.0 us)
Async XLA Ops:
  0.6 4.9 %copy-start = (f32[3,7,1024]{2,1,0:T(8,128)S(1)}, f32[3,7,1024]{2,1,0:T(8,128)}, u32[]{:S(2)}) copy-start(f32[3,7,1024]{2,1,0:T(8,128)} %f_ref.1) | copy-start | bytes 258052
  0.6 4.9 %copy-start.1 = (f32[16,1024]{1,0:T(8,128)S(1)}, f32[16,1024]{1,0:T(8,128)}, u32[]{:S(2)}) copy-start(f32[16,1024]{1,0:T(8,128)} %d_ref.1) | copy-start | bytes 196612
  0.7 4.9 %copy-start.2 = (f32[16,1024]{1,0:T(8,128)S(1)}, f32[16,1024]{1,0:T(8,128)}, u32[]{:S(2)}) copy-start(f32[16,1024]{1,0:T(8,128)} %r_ref.1) | copy-start | bytes 196612
  1.9 9.3 %collective-permute-start.3 = (bf16[24,1024]{1,0:T(8,128)(2,1)S(1)}, bf16[24,1024]{1,0:T(8,128)(2,1)S(1)}, u32[]{:S(2)}, u32[]{:S(2)}) collective-permute-start(bf16[24,1024]{1,0:T(8,128)(2,1)S(1)} %get-tuple-element.157), channel_id=1, source_target_pairs={{0,8},{8,16},{16,24},{24,32},{32,40},{40,48},{48,56},{56,64},{64,7... | collective-permute-start | bytes 147464 | tf_op jit(solution)/shard_map/ppermute | solution.py:297
  5.5 0.7 %copy-start.4 = (f32[1024]{0:T(1024)S(1)}, f32[1024]{0:T(1024)}, u32[]{:S(2)}) copy-start(f32[1024]{0:T(1024)} %param.27) | copy-start | bytes 12292
  5.5 0.7 %copy-start.3 = (f32[1024]{0:T(1024)S(1)}, f32[1024]{0:T(1024)}, u32[]{:S(2)}) copy-start(f32[1024]{0:T(1024)} %param.25) | copy-start | bytes 12292
  27.5 2.1 %copy-start.5 = (bf16[128,1024]{1,0:T(8,128)(2,1)S(1)}, bf16[128,1024]{1,0:T(8,128)(2,1)}, u32[]{:S(2)}) copy-start(bf16[128,1024]{1,0:T(8,128)(2,1)} %param.26) | copy-start | bytes 786436
  27.5 12.4 %collective-permute-start.4 = (bf16[128,128]{1,0:T(8,128)(2,1)S(1)}, bf16[128,128]{1,0:T(8,128)(2,1)S(1)}, u32[]{:S(2)}, u32[]{:S(2)}) collective-permute-start(bf16[128,128]{1,0:T(8,128)(2,1)S(1)} %get-tuple-element.171), channel_id=1, source_target_pairs={{128,384},{192,448},{129,385},{193,449},{130,386},{194,450},{131,3... | collective-permute-start | bytes 98312 | tf_op jit(solution)/shard_map/ppermute | solution.py:336
  28.3 11.6 %collective-permute-start.5 = (bf16[128,128]{1,0:T(8,128)(2,1)S(1)}, bf16[128,128]{1,0:T(8,128)(2,1)S(1)}, u32[]{:S(2)}, u32[]{:S(2)}) collective-permute-start(bf16[128,128]{1,0:T(8,128)(2,1)S(1)} %get-tuple-element.171), channel_id=1, source_target_pairs={{128,256},{192,320},{129,257},{193,321},{130,258},{194,322},{131,2... | collective-permute-start | bytes 98312 | tf_op jit(solution)/shard_map/ppermute | solution.py:336
